TPU v7x, 128 devices: a whole 4x4x4 slice. The times are simulated.
128 devices in a mesh: seq: 32 (over x, y, core), tp: 4 (over z).
Axes of the slice: x: 4, y: 4, z: 4, core: 2. Of those that a mesh axis runs over, the one named last changes fastest.
Arguments:
- states_in: bfloat16 [8192, 2048], P('seq'), may hold values from -7 to 7
- lengths: int32 [4], replicated, may hold values from 1 to 64, 128 in all
- attn_gain: float32 [2048], replicated, may hold values from 0.5 to 1.5
- w_query: bfloat16 [2048, 2048], P(None, 'tp'), may hold values from -0.125 to 0.125
- w_key: bfloat16 [2048, 2048], P(None, 'tp'), may hold values from -0.088388348 to 0.088388348
- w_value: bfloat16 [2048, 4096], P(None, 'tp'), may hold values from -0.125 to 0.125
- w_gate: bfloat16 [2048, 4096], P(None, 'tp'), may hold values from -0.125 to 0.125
- w_beta: bfloat16 [2048, 16], P(None, 'tp'), may hold values from -1 to 1
- w_alpha: bfloat16 [2048, 16], P(None, 'tp'), may hold values from -0.125 to 0.125
- decay_rate: float32 [16], P('tp'), may hold values from 4.8828125e-05 to 0.05
- decay_bias: float32 [16], P('tp'), may hold values from -2 to 1
- conv_query: float32 [4, 2048], P(None, 'tp'), may hold values from -3 to 3
- conv_key: float32 [4, 2048], P(None, 'tp'), may hold values from -3 to 3
- conv_value: float32 [4, 4096], P(None, 'tp'), may hold values from -4.5 to 4.5
- out_gain: float32 [256], replicated, may hold values from 0.5 to 1.5
- w_out: bfloat16 [4096, 2048], P('tp'), may hold values from -0.09375 to 0.09375
- final_gain: float32 [2048], replicated, may hold values from 0.5 to 1.5
- w_head: bfloat16 [2048, 32000], P(None, ('seq', 'tp')), may hold values from -0.41992188 to 0.41992188
Outputs:
- hidden: bfloat16 [8192, 2048], P('seq', 'tp')
- block_states: float32 [128, 16, 128, 256], P('seq', 'tp')
- max_logit: float32 [4], replicated
Inputs may be any that keep to these rules, and one draw needn't show every extreme that they name: Prompt lengths are counted in blocks of 64 tokens; they sum to 128 and the longest is 64.
All inputs are finite; a program needn't handle non-finite values.
Results may differ from a plain program's by a relative error of at most 0.0095.
Values may be sent and summed in bfloat16 or wider, within the bound.
No kernel may reach another device: no remote copies, remote signals or barrier semaphores. Data moves between devices by JAX's collectives and lax.ppermute only.
A program may use at most 128 MiB of HBM per device.

v0:
```python
import jax
import jax.numpy as jnp
from jax import lax
from jax.experimental import pallas as pl
from jax.experimental.pallas import tpu as pltpu
from jax.sharding import PartitionSpec as P


CONV = 4
BLOCK_LEN = 64
GROUP = 8
HALO = 16
PAD = 16
EPS = 1e-06
HIGH = lax.Precision.HIGHEST
F32 = jnp.float32
BF16 = jnp.bfloat16

VMEM = pl.BlockSpec(memory_space=pltpu.VMEM)
HBM = pl.BlockSpec(memory_space=pltpu.HBM)
SMEM = pl.BlockSpec(memory_space=pltpu.SMEM)


def whole(*dims):
    return pl.BlockSpec(dims, lambda *_: (0,) * len(dims))


def hbm(*values):
    return [pltpu.with_memory_space_constraint(value, pltpu.HBM) for value in values]


def rms_scale(values, gain):
    return values * lax.rsqrt(jnp.mean(values * values, axis=-1, keepdims=True) + EPS) * gain


def shift_groups(value, steps):
    count = lax.axis_size("seq")
    gap = steps * GROUP
    return lax.ppermute(value, "seq", [(source, source + gap) for source in range(count - gap)])


def group_exchange(value):
    count = lax.axis_size("seq")
    groups = [list(range(first, first + GROUP)) for first in range(0, count, GROUP)]
    return lax.all_to_all(value, "seq", 0, 0, axis_index_groups=groups)


def dot(a, b):
    return jnp.dot(a, b, preferred_element_type=F32)


def dot_nt(a, b):
    return lax.dot_general(a, b, (((1,), (1,)), ((), ())), preferred_element_type=F32)


def dot_tn(a, b):
    return lax.dot_general(a, b, (((0,), (0,)), ((), ())), preferred_element_type=F32)


def split(a):
    high = a.astype(BF16)
    return high, (a - high.astype(F32)).astype(BF16)


def dot3(a, b):
    a_high, a_low = split(a)
    b_high, b_low = split(b)
    return dot(a_high, b_high) + dot(a_high, b_low) + dot(a_low, b_high)


def iotas(rows, cols):
    return (
        lax.broadcasted_iota(jnp.int32, (rows, cols), 0),
        lax.broadcasted_iota(jnp.int32, (rows, cols), 1),
    )


def last_blocks(meta_ref):
    place = lax.broadcasted_iota(jnp.int32, (REQ, 1), 0)
    final = jnp.zeros((REQ, 1), jnp.int32)
    end = jnp.int32(0)
    for request in range(REQ):
        end = end + meta_ref[request]
        final = jnp.where(place == request, end - 1, final)
    return final


def norm_kernel(x_ref, gain_ref, wb_ref, wa_ref, rate_ref, bias_ref, normed_ref, scal_ref):
    tok = x_ref.shape[0]
    heads = wb_ref.shape[0]
    normed = rms_scale(x_ref[...].astype(F32), gain_ref[...]).astype(BF16)
    normed_ref[...] = normed
    beta = jax.nn.sigmoid(dot_nt(normed, wb_ref[...]))
    raw = dot_nt(normed, wa_ref[...]) + bias_ref[...]
    soft = jnp.maximum(raw, 0.0) + jnp.log1p(jnp.exp(-jnp.abs(raw)))
    log_decay = -rate_ref[...] * soft
    rows, cols = iotas(tok, tok)
    same = rows // BLOCK_LEN == cols // BLOCK_LEN
    run = jnp.dot((same & (rows >= cols)).astype(F32), log_decay, precision=HIGH, preferred_element_type=F32)
    full = jnp.dot(same.astype(F32), log_decay, precision=HIGH, preferred_element_type=F32)
    for place, value in enumerate((beta, run, jnp.exp(run), jnp.exp(full - run), jnp.exp(full))):
        scal_ref[:, place * heads : (place + 1) * heads] = value


def gate_kernel(meta_ref, normed_ref, w_gate_ref, x_ref, gate_ref, own_rows_ref, rows):
    tok = normed_ref.shape[0]
    depth = w_gate_ref.shape[0]
    lanes = own_rows_ref.shape[1]
    step = pl.program_id(0)

    @pl.when(step == 0)
    def _():
        gate_ref[...] = jnp.zeros_like(gate_ref)

    at = pl.multiple_of(step * depth, depth)
    gate_ref[...] += dot(normed_ref[:, pl.ds(at, depth)], w_gate_ref[...])

    @pl.when(step == pl.num_programs(0) - 1)
    def _():
        gate_ref[...] = jax.nn.silu(gate_ref[...])
        blocks = tok // BLOCK_LEN
        final = last_blocks(meta_ref)
        first = 0
        for ref in (gate_ref, x_ref):
            total = jnp.zeros((REQ, ref.shape[1]), F32)
            for block in range(blocks):
                end = (block + 1) * BLOCK_LEN
                line = ref[end - 8 : end, :].astype(F32)[7:8] if ref is gate_ref else ref[end - 16 : end, :].astype(F32)[15:16]
                total = total + jnp.where(final == meta_ref[REQ] * blocks + block, line, 0.0)
            for part in range(ref.shape[1] // lanes):
                rows[first : first + REQ, :] = total[:, part * lanes : (part + 1) * lanes]
                first += REQ
        own_rows_ref[...] = rows[...].astype(BF16)


def unit_lower_inverse(packed, spread, rows, cols):
    eye = (rows == cols).astype(F32)
    each = lambda fn, *lists: [fn(*items) for items in zip(*lists)]
    within = each(lambda m: jnp.where(rows // 8 == cols // 8, m, 0.0), packed)
    second = each(lambda m: dot3(m, spread(m)), within)
    fourth = each(lambda m: dot3(m, spread(m)), second)
    inverse = each(lambda m, n: dot3(eye - m, spread(eye + n)), within, second)
    inverse = each(lambda m, n: dot3(m, spread(eye + n)), inverse, fourth)
    width = 8
    while width < BLOCK_LEN:
        part = (rows // (2 * width) == cols // (2 * width)) & (rows // width != cols // width)
        left = each(lambda m, n: dot3(m, spread(jnp.where(part, n, 0.0))), inverse, packed)
        inverse = each(lambda m, n: m - dot3(n, spread(m)), inverse, left)
        width *= 2
    return inverse


def store_map(ref, at, a, b, eye):
    size = a.shape[0]
    diag = jnp.sum(jnp.where(eye, a, 0.0), axis=0, keepdims=True)
    high = diag.astype(BF16).astype(F32)
    low = diag - high
    place = lax.broadcasted_iota(jnp.int32, (PAD, size), 0)
    ref[at, :size, :] = jnp.where(eye, 0.0, a).astype(BF16)
    ref[at, size : size + PAD, :] = jnp.where(place == 0, high, jnp.where(place == 1, low, 0.0)).astype(BF16)
    ref[at, size + PAD : 2 * size + PAD, :] = b.astype(BF16)


def load_map(value, eye):
    size = value.shape[1]
    diag = value[size : size + PAD].astype(F32)
    a = value[:size].astype(F32) + jnp.where(eye, diag[0:1] + diag[1:2], 0.0)
    return a, value[size + PAD : 2 * size + PAD].astype(F32)


def maps_kernel(
    meta_ref, normed_ref, halo_ref, gain_hbm, wq_hbm, wk_hbm, wv_hbm, tq_hbm, tk_hbm, tv_hbm, scal_ref,
    maps_ref, qa_out, own_out, a_ref, b_ref, lhs, pre, qs, ks, vs, qa_ref, own_ref, a_buf, b_buf, sems,
    gain_ref, wq_ref, wk_ref, wv_ref, tq_ref, tk_ref, tv_ref, load_sems,
):
    loads = []
    for source, target in (
        (gain_hbm, gain_ref), (wq_hbm, wq_ref), (wk_hbm, wk_ref), (wv_hbm, wv_ref),
        (tq_hbm, tq_ref), (tk_hbm, tk_ref), (tv_hbm, tv_ref),
    ):
        loads.append(pltpu.make_async_copy(source, target, load_sems.at[len(loads)]))
        loads[-1].start()
    copies = []
    tok = normed_ref.shape[0]
    blocks = tok // BLOCK_LEN
    heads = qa_ref.shape[1]
    dk = qa_ref.shape[3]
    dv = own_ref.shape[3]
    rows_all = heads * BLOCK_LEN
    keep = []
    first_block = meta_ref[REQ] * blocks
    for block in range(blocks):
        offset = jnp.int32(0)
        flag = jnp.float32(1.0)
        for request in range(REQ):
            flag = jnp.where(offset == first_block + block, 0.0, flag)
            offset = offset + meta_ref[request]
        keep.append(flag)
    loads[0].wait()
    lhs[:HALO, :] = rms_scale(halo_ref[...].astype(F32), gain_ref[...]).astype(BF16)
    lhs[HALO:, :] = normed_ref[...]
    qk = heads * dk
    loads[1].wait()
    pre[:, :qk] = dot(lhs[...], wq_ref[...]).astype(BF16).astype(F32)
    loads[2].wait()
    pre[:, qk : 2 * qk] = dot(lhs[...], wk_ref[...]).astype(BF16).astype(F32)
    loads[3].wait()
    pre[:, 2 * qk :] = dot(lhs[...], wv_ref[...]).astype(BF16).astype(F32)
    for load in loads[4:]:
        load.wait()
    token = lax.broadcasted_iota(jnp.int32, (tok, 1), 0)
    masks = {}
    for lag in range(1, CONV):
        mask = jnp.ones((tok, 1), F32)
        for block in range(blocks):
            start = block * BLOCK_LEN
            mask = jnp.where((token >= start) & (token < start + lag), keep[block], mask)
        masks[lag] = mask

    def conv(first, taps_ref, at):
        total = None
        for tap in range(CONV):
            lag = CONV - 1 - tap
            part = pre[HALO - lag : HALO - lag + tok, first : first + dk] * taps_ref[tap : tap + 1, at : at + dk]
            if lag:
                part = part * masks[lag]
            total = part if total is None else total + part
        return jax.nn.silu(total)

    for head in range(heads):
        low = head * BLOCK_LEN
        for ref, base, taps_ref, scale in ((qs, 0, tq_ref, dk ** (-0.5)), (ks, qk, tk_ref, 1.0)):
            value = conv(base + head * dk, taps_ref, head * dk)
            value = value * (lax.rsqrt(jnp.sum(value * value, axis=-1, keepdims=True) + EPS) * scale)
            for block in range(blocks):
                ref[block, low : low + BLOCK_LEN, :] = value[block * BLOCK_LEN : (block + 1) * BLOCK_LEN]
        for part in range(dv // dk):
            at = head * dv + part * dk
            value = conv(2 * qk + at, tv_ref, at)
            for block in range(blocks):
                vs[block, low : low + BLOCK_LEN, part * dk : (part + 1) * dk] = value[
                    block * BLOCK_LEN : (block + 1) * BLOCK_LEN
                ]

    rows, cols = iotas(rows_all, rows_all)
    same = rows // BLOCK_LEN == cols // BLOCK_LEN
    p_rows, p_cols = iotas(BLOCK_LEN, rows_all)
    p_cols = p_cols % BLOCK_LEN
    spread = lambda value: jnp.where(same, jnp.concatenate([value] * heads, axis=0), 0.0)
    k_rows, k_cols = iotas(dk, dk)
    eye = k_rows == k_cols

    def column(place, block):
        span = slice(block * BLOCK_LEN, (block + 1) * BLOCK_LEN)
        at = place * heads
        return jnp.concatenate([scal_ref[span, at + head : at + head + 1] for head in range(heads)], axis=0)

    betas = [column(0, block) for block in range(blocks)]
    growths = [column(2, block) for block in range(blocks)]
    kbs = [ks[block].astype(BF16) for block in range(blocks)]
    p_head = lax.broadcasted_iota(jnp.int32, (BLOCK_LEN, rows_all), 1) // BLOCK_LEN
    p_lower = p_rows >= p_cols
    p_strict = p_rows > p_cols

    def choose(items):
        value = items[0]
        for head in range(1, heads):
            value = jnp.where(p_head == head, items[head], value)
        return value

    def pack(full):
        return choose([full[head * BLOCK_LEN : (head + 1) * BLOCK_LEN] for head in range(heads)])

    def beside(place, block):
        span = slice(block * BLOCK_LEN, (block + 1) * BLOCK_LEN)
        return choose([scal_ref[span, place * heads + head : place * heads + head + 1] for head in range(heads)])

    packed, scores = [], []
    for block in range(blocks):
        run = beside(1, block)
        across = jnp.sum(jnp.where(p_rows == p_cols, run, 0.0), axis=0, keepdims=True)
        decay = jnp.where(p_lower, jnp.exp(jnp.where(p_lower, run - across, 0.0)), 0.0)
        gram = pack(dot_nt(kbs[block], kbs[block]))
        packed.append(jnp.where(p_strict, beside(0, block) * gram * decay, 0.0))
        scores.append(spread(pack(dot_nt(qs[block].astype(BF16), kbs[block])) * decay).astype(BF16))
    inverses = unit_lower_inverse(packed, spread, p_rows, p_cols)
    wus = []
    for block in range(blocks):
        right = jnp.concatenate([(betas[block] * growths[block]) * ks[block], betas[block] * vs[block]], axis=1)
        wus.append(dot(spread(inverses[block]).astype(BF16), right.astype(BF16)).astype(BF16))
    q_effs, owns, tails = [], [], []
    for block in range(blocks):
        mixed = dot(scores[block], wus[block])
        q_effs.append((growths[block] * qs[block] - mixed[:, :dk]).astype(BF16))
        owns.append(mixed[:, dk:])
        tails.append((column(3, block) * ks[block]).astype(BF16))

    spans = [slice(head * BLOCK_LEN, (head + 1) * BLOCK_LEN) for head in range(heads)]
    joints = [None] * heads
    tail_place = lax.broadcasted_iota(jnp.int32, (PAD, dk), 0)
    for block in range(blocks):
        for head, span in enumerate(spans):
            grown = dot_tn(tails[block][span], wus[block][span])
            at = 4 * heads + head
            last = scal_ref[block * BLOCK_LEN : block * BLOCK_LEN + 1, at : at + 1]
            shrink, add = grown[:, :dk], grown[:, dk:]
            if block == 0:
                qa_ref[block, head] = (q_effs[block][span].astype(F32) * keep[0]).astype(BF16)
                own_ref[block, head] = owns[block][span]
                a_run = (jnp.where(eye, last, 0.0) - shrink) * keep[0]
                b_run = add
            else:
                joint = joints[head] * keep[block]
                joint_b = joint.astype(BF16)
                seen = dot(q_effs[block][span], joint_b)
                qa_ref[block, head] = seen[:, :dk].astype(BF16)
                own_ref[block, head] = seen[:, dk:] + owns[block][span]
                joint = last * joint - dot(shrink.astype(BF16), joint_b)
                a_run = joint[:, :dk]
                b_run = joint[:, dk:] + add
            joints[head] = jnp.concatenate([a_run, b_run], axis=1)
            a_buf[block, head] = a_run
            b_buf[block, head] = b_run
            if block == blocks - 1:
                for part in range(2):
                    to = 2 * head + part
                    store_map(maps_ref, to, a_run, b_run[:, part * dk : (part + 1) * dk], eye)
                    lines = []
                    for row in range(blocks):
                        lines.append(qa_ref[row, head, BLOCK_LEN - 1 :, :].astype(F32))
                    for row in range(blocks):
                        lines.append(own_ref[row, head, BLOCK_LEN - 1 :, part * dk : (part + 1) * dk])
                    tail_rows = jnp.zeros((PAD, dk), F32)
                    for row, line in enumerate(lines):
                        tail_rows = jnp.where(tail_place == row, line, tail_rows)
                    maps_ref[to, 2 * dk + PAD :, :] = tail_rows.astype(BF16)
        for place, (buf, ref) in enumerate(
            ((qa_ref, qa_out), (own_ref, own_out), (a_buf, a_ref), (b_buf, b_ref))
        ):
            copies.append(pltpu.make_async_copy(buf.at[block], ref.at[block], sems.at[place, block]))
            copies[-1].start()
    for copy in copies:
        copy.wait()


def scan_kernel(got_ref, before_ref, total_ref):
    size = got_ref.shape[2]
    rows, cols = iotas(size, size)
    eye = rows == cols
    run = None
    for member in range(GROUP):
        a, b = load_map(got_ref[member], eye)
        if run is None:
            before_ref[member] = jnp.concatenate([eye.astype(F32), jnp.zeros((size, size), F32)], axis=1)
            run = jnp.concatenate([a, b], axis=1)
        else:
            before_ref[member] = run
            run = dot3(a, run)
            run = jnp.concatenate([run[:, :size], run[:, size:] + b], axis=1)
    store_map(total_ref, 0, run[:, :size], run[:, size:], eye)


def apply_kernel(meta_ref, one_ref, two_ref, before_ref, got_ref, gain_ref, own_rows_ref, out_ref, tail):
    size = one_ref.shape[2]
    blocks = PAD // 4
    rows, cols = iotas(size, size)
    eye = rows == cols
    a, b = load_map(one_ref[0], eye)
    a_high, a_low = split(a)
    entering = dot(a_high, two_ref[...]) + dot(a_low, two_ref[...]) + b
    e_high, e_low = split(entering)
    part = meta_ref[REQ] % 2
    group = meta_ref[REQ] // GROUP
    gain = jnp.where(part == 0, gain_ref[:, :size], gain_ref[:, size:])
    final = last_blocks(meta_ref)
    kept = [jnp.zeros((REQ, size), F32), jnp.zeros((REQ, 1), F32)]
    for member in range(GROUP):
        p_high, p_low = split(before_ref[member, :, :size])
        value = dot(p_high, e_high) + dot(p_high, e_low) + dot(p_low, e_high) + before_ref[member, :, size:]
        state = value.astype(BF16)
        out_ref[member, :size, :] = state
        extra = got_ref[member, 2 * size + PAD :, :]
        out = dot(extra, state)[:blocks] + extra.astype(F32)[blocks : 2 * blocks]
        squares = jnp.sum(out * out, axis=1, keepdims=True)
        gained = out * gain
        for block in range(blocks):
            hit = final == (group * GROUP + member) * blocks + block
            for index, line in enumerate((gained[block : block + 1], squares[block : block + 1])):
                kept[index] = kept[index] + jnp.where(hit, line, 0.0)
    lane = lax.broadcasted_iota(jnp.int32, (REQ, size), 1)
    high = kept[1].astype(BF16).astype(F32)
    tail[...] = jnp.zeros_like(tail)
    tail[:REQ, :] = kept[0]
    tail[REQ : 2 * REQ, :] = jnp.where(lane == 0, high, jnp.where(lane == 1, kept[1] - high, 0.0))
    own = own_rows_ref.shape[0]
    for member in range(GROUP):
        out_ref[member, size : size + own, :] = own_rows_ref[...]
        out_ref[member, size + own :, :] = tail[...].astype(BF16)


def output_kernel(s_ref, qa_ref, own_ref, gate_ref, gain_ref, gated_ref):
    blocks, heads, block_len, dk = qa_ref.shape
    tok = blocks * block_len
    dv = own_ref.shape[3]
    for head in range(heads):
        state = jnp.concatenate([s_ref[2 * head], s_ref[2 * head + 1]], axis=1)
        out = dot(qa_ref[:, head].reshape(tok, dk), state) + own_ref[:, head].reshape(tok, dv)
        span = slice(head * dv, (head + 1) * dv)
        gated_ref[:, span] = (rms_scale(out, gain_ref[...]) * gate_ref[:, span]).astype(BF16)


def mix_kernel(meta_ref, gated_ref, w_ref, x_ref, one_ref, two_ref, three_ref, here_ref):
    step = pl.program_id(0)
    value = dot(gated_ref[...], w_ref[...])
    for place, ref in enumerate((one_ref, two_ref, three_ref)):

        @pl.when(step == place)
        def _():
            ref[...] = value.astype(BF16)

    @pl.when(step == pl.num_programs(0) - 1)
    def _():
        here_ref[...] = value + x_ref[...].astype(F32)


def rows_kernel(meta_ref, rows_ref, w_ref, send_ref, gated, sums, lines):
    step = pl.program_id(0)
    heads = pl.num_programs(0)
    dk = rows_ref.shape[2]
    share = w_ref.shape[1] // 4
    own = rows_ref.shape[1] - PAD

    @pl.when(step == 0)
    def _():
        total = rows_ref[0, :own].astype(F32)
        for member in range(1, GROUP):
            total = total + rows_ref[member, :own].astype(F32)
        lines[...] = total
        tails = [rows_ref[member, own:].astype(F32) for member in range(GROUP)]
        for head in range(heads):
            both = tails[2 * head][REQ : 2 * REQ] + tails[2 * head + 1][REQ : 2 * REQ]
            scale = lax.rsqrt(jnp.sum(both, axis=1, keepdims=True) / (2 * dk) + EPS)
            for part in range(2):
                member = 2 * head + part
                value = tails[member][:REQ] * scale * lines[member * REQ : (member + 1) * REQ, :]
                gated[head, :, part * dk : (part + 1) * dk] = value.astype(BF16)
        sums[...] = jnp.zeros_like(sums)
        for place in range(share // dk):
            at = pl.multiple_of(meta_ref[REQ + 1] * share + place * dk, dk)
            first = (GROUP + place) * REQ
            sums[:, pl.ds(at, dk)] = lines[first : first + REQ, :]

    sums[...] += dot(gated[step], w_ref[...])

    @pl.when(step == heads - 1)
    def _():
        value = sums[...].astype(BF16)
        for target in range(send_ref.shape[0]):
            send_ref[target] = value


def head_kernel(lasts_ref, gain_ref, w_ref, out_ref):
    last = jnp.sum(lasts_ref[...].astype(F32), axis=0).astype(BF16).astype(F32)
    final = rms_scale(last, gain_ref[...]).astype(BF16)
    best = jnp.max(dot(final, w_ref[...]), axis=1, keepdims=True)
    place, lane = iotas(best.shape[0], out_ref.shape[2])
    row = jnp.sum(jnp.where(place == lane, best, 0.0), axis=0, keepdims=True)
    out_ref[...] = jnp.broadcast_to(row[None], out_ref.shape)


def states_kernel(a_ref, b_ref, s_ref, out_ref):
    heads = a_ref.shape[1]
    for head in range(heads):
        state = jnp.concatenate([s_ref[2 * head], s_ref[2 * head + 1]], axis=1)
        high, low = split(a_ref[0, head])
        out_ref[0, head] = dot(high, state) + dot(low, state) + b_ref[0, head]


REQ = 4


def body(
    states_in, lengths, attn_gain, w_query, w_key, w_value, w_gate, w_beta, w_alpha, decay_rate,
    decay_bias, conv_query, conv_key, conv_value, out_gain, w_out, final_gain, w_head,
):
    tok, model = states_in.shape
    heads = decay_rate.shape[0]
    dk = w_query.shape[1] // heads
    dv = w_value.shape[1] // heads
    blocks = tok // BLOCK_LEN
    seq_count = lax.axis_size("seq")
    tp_count = lax.axis_size("tp")
    piece = lax.axis_index("seq")
    shard = lax.axis_index("tp")
    share = model // tp_count
    rows_all = heads * BLOCK_LEN
    shape = jax.ShapeDtypeStruct
    params = lambda mib: pltpu.CompilerParams(vmem_limit_bytes=mib << 20)
    meta = jnp.concatenate([lengths, piece[None], shard[None]]).astype(jnp.int32)

    halo = lax.ppermute(states_in[tok - HALO :], "seq", [(i, i + 1) for i in range(seq_count - 1)])
    gain = attn_gain[None, :]
    normed, scal = pl.pallas_call(
        norm_kernel,
        out_shape=(shape((tok, model), BF16), shape((tok, 128), F32)),
        grid=(1,),
        in_specs=[
            whole(tok, model), whole(1, model), whole(heads, model), whole(heads, model), whole(1, heads),
            whole(1, heads),
        ],
        out_specs=(whole(tok, model), whole(tok, 128)),
        compiler_params=params(24),
        name="norm_kernel",
    )(*hbm(states_in, gain, w_beta.T, w_alpha.T, decay_rate[None, :], decay_bias[None, :]))

    maps, qa, own, a_all, b_all = pl.pallas_call(
        maps_kernel,
        out_shape=(
            shape((2 * heads, 2 * dk + 2 * PAD, dk), BF16),
            pltpu.HBM((blocks, heads, BLOCK_LEN, dk), BF16),
            pltpu.HBM((blocks, heads, BLOCK_LEN, dv), F32),
            pltpu.HBM((blocks, heads, dk, dk), F32),
            pltpu.HBM((blocks, heads, dk, dv), F32),
        ),
        in_specs=[SMEM, VMEM, VMEM] + [HBM] * 7 + [VMEM],
        out_specs=(VMEM, HBM, HBM, HBM, HBM),
        scratch_shapes=[
            pltpu.VMEM((HALO + tok, model), BF16),
            pltpu.VMEM((HALO + tok, 2 * heads * dk + heads * dv), F32),
            pltpu.VMEM((blocks, rows_all, dk), F32),
            pltpu.VMEM((blocks, rows_all, dk), F32),
            pltpu.VMEM((blocks, rows_all, dv), F32),
            pltpu.VMEM((blocks, heads, BLOCK_LEN, dk), BF16),
            pltpu.VMEM((blocks, heads, BLOCK_LEN, dv), F32),
            pltpu.VMEM((blocks, heads, dk, dk), F32),
            pltpu.VMEM((blocks, heads, dk, dv), F32),
            pltpu.SemaphoreType.DMA((4, blocks)),
            pltpu.VMEM((1, model), F32),
            pltpu.VMEM(w_query.shape, BF16),
            pltpu.VMEM(w_key.shape, BF16),
            pltpu.VMEM(w_value.shape, BF16),
            pltpu.VMEM(conv_query.shape, F32),
            pltpu.VMEM(conv_key.shape, F32),
            pltpu.VMEM(conv_value.shape, F32),
            pltpu.SemaphoreType.DMA((7,)),
        ],
        compiler_params=params(40),
        name="maps_kernel",
    )(meta, normed, halo, *hbm(gain, w_query, w_key, w_value, conv_query, conv_key, conv_value), scal)

    got = group_exchange(maps)
    gate, own_rows = pl.pallas_call(
        gate_kernel,
        out_shape=(shape((tok, heads * dv), F32), shape((REQ * 3 * heads, dk), BF16)),
        grid_spec=pltpu.PrefetchScalarGridSpec(
            num_scalar_prefetch=1,
            grid=(heads,),
            in_specs=[
                whole(tok, model),
                pl.BlockSpec((model // heads, heads * dv), lambda i, m: (i, 0)),
                pl.BlockSpec((tok, share), lambda i, m: (0, m[REQ + 1])),
            ],
            out_specs=(whole(tok, heads * dv), whole(REQ * 3 * heads, dk)),
            scratch_shapes=[pltpu.VMEM((REQ * 3 * heads, dk), F32)],
        ),
        compiler_params=params(24),
        name="gate_kernel",
    )(meta, *hbm(normed, w_gate, states_in))
    got, gate, own_rows = lax.optimization_barrier((got, gate, own_rows))
    before, total = pl.pallas_call(
        scan_kernel,
        out_shape=(shape((GROUP, dk, 2 * dk), F32), shape((1, 2 * dk + PAD, dk), BF16)),
        in_specs=[VMEM],
        out_specs=(VMEM,) * 2,
        compiler_params=params(16),
        name="scan_kernel",
    )(got)
    one_back = shift_groups(total, 1)
    two_back = shift_groups(total[0, dk + PAD :], 2)
    rows_len = own_rows.shape[0] + PAD
    incoming = pl.pallas_call(
        apply_kernel,
        out_shape=shape((GROUP, dk + rows_len, dk), BF16),
        in_specs=[SMEM] + [VMEM] * 6,
        out_specs=VMEM,
        scratch_shapes=[pltpu.VMEM((PAD, dk), F32)],
        compiler_params=params(16),
        name="apply_kernel",
    )(meta, one_back, two_back, before, got, out_gain[None, :], own_rows)
    s_in = group_exchange(incoming)

    groups = seq_count // GROUP
    joint = [
        [(GROUP * group + member) * tp_count + column for group in range(groups) for column in range(tp_count)]
        for member in range(GROUP)
    ]
    sends = pl.pallas_call(
        rows_kernel,
        out_shape=shape((groups * tp_count, REQ, model), BF16),
        grid_spec=pltpu.PrefetchScalarGridSpec(
            num_scalar_prefetch=1,
            grid=(heads,),
            in_specs=[
                pl.BlockSpec((GROUP, rows_len, dk), lambda i, m: (0, dk // rows_len, 0)),
                pl.BlockSpec((dv, model), lambda i, m: (i, 0)),
            ],
            out_specs=whole(groups * tp_count, REQ, model),
            scratch_shapes=[
                pltpu.VMEM((heads, REQ, dv), BF16),
                pltpu.VMEM((REQ, model), F32),
                pltpu.VMEM((rows_len - PAD, dk), F32),
            ],
        ),
        compiler_params=params(24),
        name="rows_kernel",
    )(meta, *hbm(s_in, w_out))
    sends, s_after = lax.optimization_barrier((sends, s_in))
    lasts = lax.all_to_all(sends, ("seq", "tp"), 0, 0, axis_index_groups=joint)
    gated = pl.pallas_call(
        output_kernel,
        out_shape=shape((tok, heads * dv), BF16),
        grid=(1,),
        in_specs=[
            whole(2 * heads, dk, dk),
            whole(blocks, heads, BLOCK_LEN, dk),
            whole(blocks, heads, BLOCK_LEN, dv),
            whole(tok, heads * dv),
            whole(1, dv),
        ],
        out_specs=whole(tok, heads * dv),
        compiler_params=params(24),
        name="output_kernel",
    )(s_after, qa, own, gate, out_gain[None, :])

    turn = lambda i, m: (m[REQ + 1] + i + 1) % tp_count
    one, two, three, here = pl.pallas_call(
        mix_kernel,
        out_shape=(shape((tok, share), BF16),) * 3 + (shape((tok, share), F32),),
        grid_spec=pltpu.PrefetchScalarGridSpec(
            num_scalar_prefetch=1,
            grid=(tp_count,),
            in_specs=[
                whole(tok, heads * dv),
                pl.BlockSpec((heads * dv, share), lambda i, m: (0, turn(i, m))),
                pl.BlockSpec((tok, share), lambda i, m: (0, m[REQ + 1])),
            ],
            out_specs=(whole(tok, share),) * 4,
        ),
        compiler_params=params(24),
        name="mix_kernel",
    )(meta, gated, *hbm(w_out, states_in))

    rings = [[(i, (i + offset) % tp_count) for i in range(tp_count)] for offset in range(1, tp_count)]
    spread = pl.pallas_call(
        head_kernel,
        out_shape=shape((seq_count * tp_count, 1, 128), F32),
        grid=(1,),
        in_specs=[whole(groups * tp_count, REQ, model), whole(1, model), whole(*w_head.shape)],
        out_specs=whole(seq_count * tp_count, 1, 128),
        compiler_params=params(24),
        name="head_kernel",
    )(lasts, final_gain[None, :], w_head)
    spread, s_late = lax.optimization_barrier((spread, s_after))
    bests = lax.all_to_all(spread, ("seq", "tp"), 0, 0)
    block_states = pl.pallas_call(
        states_kernel,
        out_shape=shape((blocks, heads, dk, dv), F32),
        grid=(blocks,),
        in_specs=[
            pl.BlockSpec((1, heads, dk, dk), lambda i: (i, 0, 0, 0)),
            pl.BlockSpec((1, heads, dk, dv), lambda i: (i, 0, 0, 0)),
            pl.BlockSpec((2 * heads, dk, dk), lambda i: (0, 0, 0)),
        ],
        out_specs=pl.BlockSpec((1, heads, dk, dv), lambda i: (i, 0, 0, 0)),
        compiler_params=params(16),
        name="states_kernel",
    )(*hbm(a_all, b_all, s_late))

    mixed = here
    for ring, value in zip(rings, (one, two, three)):
        mixed = mixed + lax.ppermute(value, "tp", ring).astype(F32)
    hidden = mixed.astype(BF16)
    max_logit = jnp.max(bests[:, 0, :REQ], axis=0)
    return (hidden, block_states, max_logit)


def solution(mesh):
    return jax.shard_map(
        body,
        mesh=mesh,
        in_specs=(
            P("seq", None), P(), P(), P(None, "tp"), P(None, "tp"), P(None, "tp"), P(None, "tp"),
            P(None, "tp"), P(None, "tp"), P("tp"), P("tp"), P(None, "tp"), P(None, "tp"), P(None, "tp"),
            P(), P("tp", None), P(), P(None, ("seq", "tp")),
        ),
        out_specs=(P("seq", "tp"), P("seq", "tp", None, None), P()),
        check_vma=False,
    )
```

profile of v0, /device:TPU:1, one launch (start us, length us, event | category | flops | bytes accessed | tf_op | source)
XLA Modules:
  0.0 113.1 jit_solution(10417395983125727521)
XLA Ops:
  0.6 0.8 slice.9
  1.5 4.6 %collective-permute-start = (bf16[16,2048]{1,0:T(8,128)(2,1)S(1)}, bf16[16,2048]{1,0:T(8,128)(2,1)S(1)}, u32[]{:S(2)}, u32[]{:S(2)}) collective-permute-start(bf16[16,2048]{1,0:T(8,128)(2,1)S(1)} %slice.9), channel_id=1, source_target_pairs={{0,4},{4,8},{8,12},{12,16},{16,20},{20,24},{24,28},{28,32},{32,36}... | collective-permute-start | bytes 196616 | tf_op jit(solution)/shard_map/ppermute | solution.py:501
  6.1 3.0 %norm_kernel.1 = (bf16[256,2048]{1,0:T(8,128)(2,1)S(1)}, f32[256,128]{1,0:T(8,128)S(1)}) custom-call(bf16[256,2048]{1,0:T(8,128)(2,1)} %x_ref.5, f32[1,2048]{1,0:T(1,128)} %bitcast.14, bf16[4,2048]{1,0:T(4,128)(2,1)} %bitcast.16, bf16[4,2048]{1,0:T(4,128)(2,1)} %bitcast.17, f32[1,4]{1,0:T(1,128)} %bitcast.18, f32[1,4]{1,0:T(1,128)} %bitcast.19), custom_call_target="tpu_custom_call" | custom-call | tf_op jit(solution)/shard_map/norm_kernel/pallas_call | solution.py:503
  9.1 0.0 copy-start.1
  9.1 0.8 pad_add_fusion.meta_ref
  9.8 0.0 collective-permute-done.halo_ref
  9.8 14.8 %maps_kernel.1 = (bf16[8,288,128]{2,1,0:T(8,128)(2,1)}, bf16[4,4,64,128]{3,2,1,0:T(8,128)(2,1)}, f32[4,4,64,256]{3,2,1,0:T(8,128)}, f32[4,4,128,128]{3,2,1,0:T(8,128)}, f32[4,4,128,256]{3,2,1,0:T(8,128)}) custom-call(s32[6]{0:T(128)S(1)} %pad_add_fusion.meta_ref, bf16[256,2048]{1,0:T(8,128)(2,1)S(1)} %get-tuple-element.25.normed_ref, ...), custom_call_target="tpu_custom_call" | custom-call | tf_op jit(solution)/shard_map/maps_kernel/pallas_call | solution.py:516
  24.6 0.0 copy-done.1
  24.6 4.3 %all-to-all-start = ((bf16[8,288,128]{2,1,0:T(8,128)(2,1)}), bf16[8,288,128]{2,1,0:T(8,128)(2,1)S(1)}, u32[]{:S(2)}, u32[]{:S(2)}) async-start(bf16[8,288,128]{2,1,0:T(8,128)(2,1)} %get-tuple-element.27), calls=%async_computation | async-start | bytes 1179648 | tf_op jit(solution)/shard_map/all_to_all | solution.py:45
  28.9 0.0 copy-start.6
  28.9 5.1 %gate_kernel.1 = (f32[256,1024]{1,0:T(8,128)S(1)}, bf16[48,128]{1,0:T(8,128)(2,1)S(1)}) custom-call(s32[6]{0:T(128)S(1)} %pad_add_fusion.meta_ref, bf16[256,2048]{1,0:T(8,128)(2,1)} %copy-done.1, bf16[2048,1024]{1,0:T(8,128)(2,1)} %w_gate_ref.1, bf16[256,2048]{1,0:T(8,128)(2,1)} %x_ref.5), custom_call_target="tpu_custom_call" | custom-call | tf_op jit(solution)/shard_map/gate_kernel/pallas_call | solution.py:552
  34.1 4.9 %all-to-all-done.got_ref = bf16[8,288,128]{2,1,0:T(8,128)(2,1)S(1)} async-done(((bf16[8,288,128]{2,1,0:T(8,128)(2,1)}), bf16[8,288,128]{2,1,0:T(8,128)(2,1)S(1)}, u32[]{:S(2)}, u32[]{:S(2)}) %all-to-all-start) | async-done | bytes 589856 | tf_op jit(solution)/shard_map/all_to_all | solution.py:45
  39.0 1.5 %scan_kernel.1 = (f32[8,128,256]{2,1,0:T(8,128)S(1)}, bf16[1,272,128]{2,1,0:T(8,128)(2,1)S(1)}) custom-call(bf16[8,288,128]{2,1,0:T(8,128)(2,1)S(1)} %all-to-all-done.got_ref), custom_call_target="tpu_custom_call" | custom-call | tf_op jit(solution)/shard_map/scan_kernel/pallas_call | solution.py:570
  40.5 3.1 %collective-permute-start.1 = (bf16[1,272,128]{2,1,0:T(8,128)(2,1)S(1)}, bf16[1,272,128]{2,1,0:T(8,128)(2,1)S(1)}, u32[]{:S(2)}, u32[]{:S(2)}) collective-permute-start(bf16[1,272,128]{2,1,0:T(8,128)(2,1)S(1)} %get-tuple-element.31), channel_id=1, source_target_pairs={{0,32},{4,36},{8,40},{12,44},{16,48},{20,52},{24,56},{28,60},{32,6... | collective-permute-start | bytes 208904 | tf_op jit(solution)/shard_map/ppermute | solution.py:39
  43.7 4.5 %collective-permute-start.2 = (bf16[128,128]{1,0:T(8,128)(2,1)S(1)}, bf16[128,128]{1,0:T(8,128)(2,1)S(1)}, u32[]{:S(2)}, u32[]{:S(2)}) collective-permute-start(bf16[128,128]{1,0:T(8,128)(2,1)S(1)} %slice_bitcast_fusion), channel_id=1, source_target_pairs={{0,64},{4,68},{8,72},{12,76},{16,80},{20,84},{24,88},{28,92},{32,9... | collective-permute-start | bytes 98312 | tf_op jit(solution)/shard_map/ppermute | solution.py:39
  48.2 0.8 collective-permute-done.2.two_ref
  49.0 0.0 collective-permute-done.1.one_ref
  49.0 0.0 copy-done.6
  49.0 2.4 %apply_kernel.1 = bf16[8,192,128]{2,1,0:T(8,128)(2,1)S(1)} custom-call(s32[6]{0:T(128)S(1)} %pad_add_fusion.meta_ref, bf16[1,272,128]{2,1,0:T(8,128)(2,1)S(1)} %collective-permute-done.1.one_ref, bf16[128,128]{1,0:T(8,128)(2,1)S(1)} %collective-permute-done.2.two_ref, f32[8,128,256]{2,1,0:T(8,128)S(1)} %get-tuple-element.32.before_ref, ...), custom_call_target="tpu_custom_call" | custom-call | tf_op jit(solution)/shard_map/apply_kernel/pallas_call | solution.py:581
  51.4 13.2 %all_to_all.20.rows_ref.s_ref = bf16[8,192,128]{2,1,0:T(8,128)(2,1)} all-to-all(bf16[8,192,128]{2,1,0:T(8,128)(2,1)S(1)} %apply_kernel.1), channel_id=1, replica_groups={{0,4,8,12,16,20,24,28},{32,36,40,44,48,52,56,60},{64,68,72,76,80,84,88,..., dimensions={0} | all-to-all | bytes 786432 | tf_op jit(solution)/shard_map/all_to_all | solution.py:45
  64.6 0.0 copy-start
  64.6 0.0 copy-start.3
  64.6 0.0 copy-start.4
  64.6 4.0 %rows_kernel.1 = bf16[16,4,2048]{2,1,0:T(4,128)(2,1)S(1)} custom-call(s32[6]{0:T(128)S(1)} %pad_add_fusion.meta_ref, bf16[8,192,128]{2,1,0:T(8,128)(2,1)} %all_to_all.20.rows_ref.s_ref, bf16[1024,2048]{1,0:T(8,128)(2,1)} %w_ref.4), custom_call_target="tpu_custom_call" | custom-call | tf_op jit(solution)/shard_map/rows_kernel/pallas_call | solution.py:597
  68.7 0.0 copy-done
  68.7 0.0 copy-done.3
  68.7 0.0 copy-done.4
  68.7 0.5 output_kernel.1.gated_ref
  69.1 0.0 copy-start.2
  69.2 0.0 copy-start.5
  69.2 4.6 %mix_kernel.1 = (bf16[256,512]{1,0:T(8,128)(2,1)S(1)}, bf16[256,512]{1,0:T(8,128)(2,1)S(1)}, bf16[256,512]{1,0:T(8,128)(2,1)S(1)}, f32[256,512]{1,0:T(8,128)S(1)}) custom-call(s32[6]{0:T(128)S(1)} %pad_add_fusion.meta_ref, bf16[256,1024]{1,0:T(8,128)(2,1)S(1)} %output_kernel.1.gated_ref, bf16[1024,2048]{1,0:T(8,128)(2,1)} %w_ref.4, bf16[256,2048]{1,0:T(8,128)(2,1)} %x_ref.5), custom_call_target="tpu_custom_call" | custom-call | tf_op jit(solution)/shard_map/mix_kernel/pallas_call | solution.py:636
  73.8 1.7 %collective-permute-start.3 = (bf16[256,512]{1,0:T(8,128)(2,1)S(1)}, bf16[256,512]{1,0:T(8,128)(2,1)S(1)}, u32[]{:S(2)}, u32[]{:S(2)}) collective-permute-start(bf16[256,512]{1,0:T(8,128)(2,1)S(1)} %get-tuple-element.39), channel_id=1, source_target_pairs={{0,1},{1,2},{2,3},{3,0},{4,5},{5,6},{6,7},{7,4},{8,9},{9,10},{10,1... | collective-permute-start | bytes 786440 | tf_op jit(solution)/shard_map/ppermute | solution.py:681
  75.5 3.3 %collective-permute-start.4 = (bf16[256,512]{1,0:T(8,128)(2,1)S(1)}, bf16[256,512]{1,0:T(8,128)(2,1)S(1)}, u32[]{:S(2)}, u32[]{:S(2)}) collective-permute-start(bf16[256,512]{1,0:T(8,128)(2,1)S(1)} %get-tuple-element.40), channel_id=1, source_target_pairs={{0,2},{1,3},{2,0},{3,1},{4,6},{5,7},{6,4},{7,5},{8,10},{9,11},{10,... | collective-permute-start | bytes 786440 | tf_op jit(solution)/shard_map/ppermute | solution.py:681
  78.8 0.7 collective-permute-start.5
  79.6 13.6 %all_to_all.21.lasts_ref = bf16[16,4,2048]{2,1,0:T(4,128)(2,1)S(1)} all-to-all(bf16[16,4,2048]{2,1,0:T(4,128)(2,1)S(1)} %rows_kernel.1), channel_id=1, replica_groups={{0,1,2,3,32,33,34,35,64,65,66,67,96,97,98,99},{4,5,6,7,36,37,38,39,68,6..., dimensions={0} | all-to-all | bytes 524288 | tf_op jit(solution)/shard_map/all_to_all | solution.py:618
  93.1 0.0 copy-done.2
  93.1 0.0 copy-done.5
  93.1 1.2 %head_kernel.1 = f32[128,1,128]{2,1,0:T(1,128)} custom-call(bf16[16,4,2048]{2,1,0:T(4,128)(2,1)S(1)} %all_to_all.21.lasts_ref, f32[1,2048]{1,0:T(1,128)S(1)} %bitcast.11, bf16[2048,250]{1,0:T(8,128)(2,1)S(1)} %copy-done.2), custom_call_target="tpu_custom_call" | custom-call | tf_op jit(solution)/shard_map/head_kernel/pallas_call | solution.py:654
  94.3 8.4 %all-to-all-start.3 = ((f32[128,1,128]{2,1,0:T(1,128)}), f32[128,1,128]{2,1,0:T(1,128)S(1)}, u32[]{:S(2)}, u32[]{:S(2)}) async-start(f32[128,1,128]{2,1,0:T(1,128)} %head_kernel.1), calls=%async_computation.3 | async-start | bytes 131072 | tf_op jit(solution)/shard_map/all_to_all | solution.py:664
  102.7 4.6 %states_kernel.1 = f32[4,4,128,256]{3,2,1,0:T(8,128)} custom-call(f32[4,4,128,128]{3,2,1,0:T(8,128)} %get-tuple-element.42.a_ref, f32[4,4,128,256]{3,2,1,0:T(8,128)} %get-tuple-element.43.b_ref, bf16[8,192,128]{2,1,0:T(8,128)(2,1)} %all_to_all.20.rows_ref.s_ref), custom_call_target="tpu_custom_call" | custom-call | tf_op jit(solution)/shard_map/states_kernel/pallas_call | solution.py:665
  107.2 0.0 collective-permute-done.3
  107.2 0.0 collective-permute-done.4
  107.2 0.0 collective-permute-done.5
  107.2 0.8 add_convert_fusion
  108.1 4.3 %all-to-all-done.3 = f32[128,1,128]{2,1,0:T(1,128)S(1)} async-done(((f32[128,1,128]{2,1,0:T(1,128)}), f32[128,1,128]{2,1,0:T(1,128)S(1)}, u32[]{:S(2)}, u32[]{:S(2)}) %all-to-all-start.3) | async-done | bytes 65568 | tf_op jit(solution)/shard_map/all_to_all | solution.py:664
  112.4 0.7 slice_reduce_fusion
  (1 shorter events, 0.0 us)
Async XLA Ops:
  1.5 8.4 %collective-permute-start = (bf16[16,2048]{1,0:T(8,128)(2,1)S(1)}, bf16[16,2048]{1,0:T(8,128)(2,1)S(1)}, u32[]{:S(2)}, u32[]{:S(2)}) collective-permute-start(bf16[16,2048]{1,0:T(8,128)(2,1)S(1)} %slice.9), channel_id=1, source_target_pairs={{0,4},{4,8},{8,12},{12,16},{16,20},{20,24},{24,28},{28,32},{32,36}... | collective-permute-start | bytes 196616 | tf_op jit(solution)/shard_map/ppermute | solution.py:501
  9.1 15.6 %copy-start.1 = (bf16[256,2048]{1,0:T(8,128)(2,1)}, bf16[256,2048]{1,0:T(8,128)(2,1)S(1)}, u32[]{:S(2)}) copy-start(bf16[256,2048]{1,0:T(8,128)(2,1)S(1)} %get-tuple-element.25.normed_ref) | copy-start | bytes 3145732
  24.6 14.4 %all-to-all-start = ((bf16[8,288,128]{2,1,0:T(8,128)(2,1)}), bf16[8,288,128]{2,1,0:T(8,128)(2,1)S(1)}, u32[]{:S(2)}, u32[]{:S(2)}) async-start(bf16[8,288,128]{2,1,0:T(8,128)(2,1)} %get-tuple-element.27), calls=%async_computation | async-start | bytes 1179648 | tf_op jit(solution)/shard_map/all_to_all | solution.py:45
  28.9 20.1 %copy-start.6 = (f32[256]{0:T(256)S(1)}, f32[256]{0:T(256)}, u32[]{:S(2)}) copy-start(f32[256]{0:T(256)} %param.32) | copy-start | bytes 3076
  40.5 8.5 %collective-permute-start.1 = (bf16[1,272,128]{2,1,0:T(8,128)(2,1)S(1)}, bf16[1,272,128]{2,1,0:T(8,128)(2,1)S(1)}, u32[]{:S(2)}, u32[]{:S(2)}) collective-permute-start(bf16[1,272,128]{2,1,0:T(8,128)(2,1)S(1)} %get-tuple-element.31), channel_id=1, source_target_pairs={{0,32},{4,36},{8,40},{12,44},{16,48},{20,52},{24,56},{28,60},{32,6... | collective-permute-start | bytes 208904 | tf_op jit(solution)/shard_map/ppermute | solution.py:39
  43.7 5.4 %collective-permute-start.2 = (bf16[128,128]{1,0:T(8,128)(2,1)S(1)}, bf16[128,128]{1,0:T(8,128)(2,1)S(1)}, u32[]{:S(2)}, u32[]{:S(2)}) collective-permute-start(bf16[128,128]{1,0:T(8,128)(2,1)S(1)} %slice_bitcast_fusion), channel_id=1, source_target_pairs={{0,64},{4,68},{8,72},{12,76},{16,80},{20,84},{24,88},{28,92},{32,9... | collective-permute-start | bytes 98312 | tf_op jit(solution)/shard_map/ppermute | solution.py:39
  64.6 4.0 %copy-start = (bf16[8,192,128]{2,1,0:T(8,128)(2,1)S(1)}, bf16[8,192,128]{2,1,0:T(8,128)(2,1)}, u32[]{:S(2)}) copy-start(bf16[8,192,128]{2,1,0:T(8,128)(2,1)} %all_to_all.20.rows_ref.s_ref) | copy-start | bytes 1179652
  64.6 4.0 %copy-start.3 = (f32[4,4,64,256]{3,2,1,0:T(8,128)S(1)}, f32[4,4,64,256]{3,2,1,0:T(8,128)}, u32[]{:S(2)}) copy-start(f32[4,4,64,256]{3,2,1,0:T(8,128)} %get-tuple-element.36.own_ref) | copy-start | bytes 3145732
  64.6 4.0 %copy-start.4 = (bf16[4,4,64,128]{3,2,1,0:T(8,128)(2,1)S(1)}, bf16[4,4,64,128]{3,2,1,0:T(8,128)(2,1)}, u32[]{:S(2)}) copy-start(bf16[4,4,64,128]{3,2,1,0:T(8,128)(2,1)} %get-tuple-element.35.qa_ref) | copy-start | bytes 786436
  69.1 24.0 %copy-start.2 = (bf16[2048,250]{1,0:T(8,128)(2,1)S(1)}, bf16[2048,250]{1,0:T(8,128)(2,1)}, u32[]{:S(2)}) copy-start(bf16[2048,250]{1,0:T(8,128)(2,1)} %w_ref.5) | copy-start | bytes 3072004
  69.2 24.0 %copy-start.5 = (f32[2048]{0:T(1024)S(1)}, f32[2048]{0:T(1024)}, u32[]{:S(2)}) copy-start(f32[2048]{0:T(1024)} %param.34) | copy-start | bytes 24580
  73.8 33.4 %collective-permute-start.3 = (bf16[256,512]{1,0:T(8,128)(2,1)S(1)}, bf16[256,512]{1,0:T(8,128)(2,1)S(1)}, u32[]{:S(2)}, u32[]{:S(2)}) collective-permute-start(bf16[256,512]{1,0:T(8,128)(2,1)S(1)} %get-tuple-element.39), channel_id=1, source_target_pairs={{0,1},{1,2},{2,3},{3,0},{4,5},{5,6},{6,7},{7,4},{8,9},{9,10},{10,1... | collective-permute-start | bytes 786440 | tf_op jit(solution)/shard_map/ppermute | solution.py:681
  75.5 31.7 %collective-permute-start.4 = (bf16[256,512]{1,0:T(8,128)(2,1)S(1)}, bf16[256,512]{1,0:T(8,128)(2,1)S(1)}, u32[]{:S(2)}, u32[]{:S(2)}) collective-permute-start(bf16[256,512]{1,0:T(8,128)(2,1)S(1)} %get-tuple-element.40), channel_id=1, source_target_pairs={{0,2},{1,3},{2,0},{3,1},{4,6},{5,7},{6,4},{7,5},{8,10},{9,11},{10,... | collective-permute-start | bytes 786440 | tf_op jit(solution)/shard_map/ppermute | solution.py:681
  78.8 28.4 %collective-permute-start.5 = (bf16[256,512]{1,0:T(8,128)(2,1)S(1)}, bf16[256,512]{1,0:T(8,128)(2,1)S(1)}, u32[]{:S(2)}, u32[]{:S(2)}) collective-permute-start(bf16[256,512]{1,0:T(8,128)(2,1)S(1)} %get-tuple-element.41), channel_id=1, source_target_pairs={{0,3},{1,0},{2,1},{3,2},{4,7},{5,4},{6,5},{7,6},{8,11},{9,8},{10,9... | collective-permute-start | bytes 786440 | tf_op jit(solution)/shard_map/ppermute | solution.py:681
  94.3 18.1 %all-to-all-start.3 = ((f32[128,1,128]{2,1,0:T(1,128)}), f32[128,1,128]{2,1,0:T(1,128)S(1)}, u32[]{:S(2)}, u32[]{:S(2)}) async-start(f32[128,1,128]{2,1,0:T(1,128)} %head_kernel.1), calls=%async_computation.3 | async-start | bytes 131072 | tf_op jit(solution)/shard_map/all_to_all | solution.py:664
where the time goes:
time: 114 us; the launch traced here: 113 us
  Pallas kernels  41.6 us (36%)
  starting transfers between devices  30.6 us (27%)
  blocking collectives  26.8 us (24%)
  waiting for transfers between devices  10.1 us (9%)
  other arithmetic  2.26 us (2%)
    pallas_call x1, Pallas kernels, body(): pl.pallas_call(maps_kernel, out_shape=(shape((2 * heads, 2 * dk + 2 * PAD...  14.8 us
    all_to_all x1, blocking collectives, body(): lasts = lax.all_to_all(sends, ('seq', 'tp'), 0, 0, axis_index_groups=joint)  13.6 us
    all_to_all x1, blocking collectives, group_exchange(): return lax.all_to_all(value, 'seq', 0, 0, axis_index_groups=groups)  13.2 us
    all_to_all x1, starting transfers between devices, body(): bests = lax.all_to_all(spread, ('seq', 'tp'), 0, 0)  8.35 us
    ppermute x2, starting transfers between devices, shift_groups(): lax.ppermute(value, 'seq', [(source, source + gap) for source in range(co...  7.66 us
    ppermute x3, starting transfers between devices, body(): mixed = mixed + lax.ppermute(value, 'tp', ring).astype(F32)  5.75 us
    pallas_call x1, Pallas kernels, body(): pl.pallas_call(gate_kernel, out_shape=(shape((tok, heads * dv), F32), sha...  5.11 us
    all_to_all x1, waiting for transfers between devices, group_exchange(): return lax.all_to_all(value, 'seq', 0, 0, axis_index_groups=groups)  4.93 us
  transfers between devices with their start and end apart: 8, of which 3 were waited for; matrix products, arithmetic and copies ran while one was open for 1% of the time, Pallas kernels for 12%

commit v1 on v0

--- a/solution.py
+++ b/solution.py
@@ -85,11 +85,9 @@
     return final
 
 
-def norm_kernel(x_ref, gain_ref, wb_ref, wa_ref, rate_ref, bias_ref, normed_ref, scal_ref):
-    tok = x_ref.shape[0]
+def fill_scalars(normed, wb_ref, wa_ref, rate_ref, bias_ref, scal_ref):
+    tok = normed.shape[0]
     heads = wb_ref.shape[0]
-    normed = rms_scale(x_ref[...].astype(F32), gain_ref[...]).astype(BF16)
-    normed_ref[...] = normed
     beta = jax.nn.sigmoid(dot_nt(normed, wb_ref[...]))
     raw = dot_nt(normed, wa_ref[...]) + bias_ref[...]
     soft = jnp.maximum(raw, 0.0) + jnp.log1p(jnp.exp(-jnp.abs(raw)))
@@ -169,19 +167,22 @@
 
 
 def maps_kernel(
-    meta_ref, normed_ref, halo_ref, gain_hbm, wq_hbm, wk_hbm, wv_hbm, tq_hbm, tk_hbm, tv_hbm, scal_ref,
-    maps_ref, qa_out, own_out, a_ref, b_ref, lhs, pre, qs, ks, vs, qa_ref, own_ref, a_buf, b_buf, sems,
-    gain_ref, wq_ref, wk_ref, wv_ref, tq_ref, tk_ref, tv_ref, load_sems,
+    meta_ref, halo_ref, x_hbm, gain_hbm, wb_hbm, wa_hbm, rate_hbm, bias_hbm, wq_hbm, wk_hbm, wv_hbm,
+    tq_hbm, tk_hbm, tv_hbm,
+    maps_ref, normed_out, qa_out, own_out, a_ref, b_ref, lhs, pre, qs, ks, vs, qa_ref, own_ref, a_buf, b_buf, sems,
+    scal_ref, x_ref, gain_ref, wb_ref, wa_ref, rate_ref, bias_ref, wq_ref, wk_ref, wv_ref,
+    tq_ref, tk_ref, tv_ref, load_sems, normed_sem,
 ):
     loads = []
     for source, target in (
-        (gain_hbm, gain_ref), (wq_hbm, wq_ref), (wk_hbm, wk_ref), (wv_hbm, wv_ref),
-        (tq_hbm, tq_ref), (tk_hbm, tk_ref), (tv_hbm, tv_ref),
+        (x_hbm, x_ref), (gain_hbm, gain_ref), (wq_hbm, wq_ref), (wk_hbm, wk_ref), (wb_hbm, wb_ref),
+        (wa_hbm, wa_ref), (rate_hbm, rate_ref), (bias_hbm, bias_ref), (tq_hbm, tq_ref), (tk_hbm, tk_ref),
+        (wv_hbm, wv_ref), (tv_hbm, tv_ref),
     ):
         loads.append(pltpu.make_async_copy(source, target, load_sems.at[len(loads)]))
         loads[-1].start()
     copies = []
-    tok = normed_ref.shape[0]
+    tok = x_ref.shape[0]
     blocks = tok // BLOCK_LEN
     heads = qa_ref.shape[1]
     dk = qa_ref.shape[3]
@@ -197,17 +198,18 @@
             offset = offset + meta_ref[request]
         keep.append(flag)
     loads[0].wait()
+    loads[1].wait()
     lhs[:HALO, :] = rms_scale(halo_ref[...].astype(F32), gain_ref[...]).astype(BF16)
-    lhs[HALO:, :] = normed_ref[...]
+    lhs[HALO:, :] = rms_scale(x_ref[...].astype(F32), gain_ref[...]).astype(BF16)
+    copies.append(pltpu.make_async_copy(lhs.at[pl.ds(HALO, tok), :], normed_out, normed_sem.at[0]))
+    copies[-1].start()
     qk = heads * dk
-    loads[1].wait()
+    loads[2].wait()
     pre[:, :qk] = dot(lhs[...], wq_ref[...]).astype(BF16).astype(F32)
-    loads[2].wait()
+    for load in loads[3:10]:
+        load.wait()
     pre[:, qk : 2 * qk] = dot(lhs[...], wk_ref[...]).astype(BF16).astype(F32)
-    loads[3].wait()
-    pre[:, 2 * qk :] = dot(lhs[...], wv_ref[...]).astype(BF16).astype(F32)
-    for load in loads[4:]:
-        load.wait()
+    fill_scalars(lhs[HALO:, :], wb_ref, wa_ref, rate_ref, bias_ref, scal_ref)
     token = lax.broadcasted_iota(jnp.int32, (tok, 1), 0)
     masks = {}
     for lag in range(1, CONV):
@@ -234,6 +236,11 @@
             value = value * (lax.rsqrt(jnp.sum(value * value, axis=-1, keepdims=True) + EPS) * scale)
             for block in range(blocks):
                 ref[block, low : low + BLOCK_LEN, :] = value[block * BLOCK_LEN : (block + 1) * BLOCK_LEN]
+    for load in loads[10:]:
+        load.wait()
+    pre[:, 2 * qk :] = dot(lhs[...], wv_ref[...]).astype(BF16).astype(F32)
+    for head in range(heads):
+        low = head * BLOCK_LEN
         for part in range(dv // dk):
             at = head * dv + part * dk
             value = conv(2 * qk + at, tv_ref, at)
@@ -423,40 +430,48 @@
         here_ref[...] = value + x_ref[...].astype(F32)
 
 
-def rows_kernel(meta_ref, rows_ref, w_ref, send_ref, gated, sums, lines):
-    step = pl.program_id(0)
-    heads = pl.num_programs(0)
+def rows_kernel(meta_ref, s_hbm, w_hbm, send_ref, rows_ref, w_ref, sums, lines, sems):
     dk = rows_ref.shape[2]
+    dv = 2 * dk
+    heads = w_ref.shape[0] // dv
     share = w_ref.shape[1] // 4
     own = rows_ref.shape[1] - PAD
-
-    @pl.when(step == 0)
-    def _():
-        total = rows_ref[0, :own].astype(F32)
-        for member in range(1, GROUP):
-            total = total + rows_ref[member, :own].astype(F32)
-        lines[...] = total
-        tails = [rows_ref[member, own:].astype(F32) for member in range(GROUP)]
-        for head in range(heads):
-            both = tails[2 * head][REQ : 2 * REQ] + tails[2 * head + 1][REQ : 2 * REQ]
-            scale = lax.rsqrt(jnp.sum(both, axis=1, keepdims=True) / (2 * dk) + EPS)
-            for part in range(2):
-                member = 2 * head + part
-                value = tails[member][:REQ] * scale * lines[member * REQ : (member + 1) * REQ, :]
-                gated[head, :, part * dk : (part + 1) * dk] = value.astype(BF16)
-        sums[...] = jnp.zeros_like(sums)
-        for place in range(share // dk):
-            at = pl.multiple_of(meta_ref[REQ + 1] * share + place * dk, dk)
-            first = (GROUP + place) * REQ
-            sums[:, pl.ds(at, dk)] = lines[first : first + REQ, :]
-
-    sums[...] += dot(gated[step], w_ref[...])
-
-    @pl.when(step == heads - 1)
-    def _():
-        value = sums[...].astype(BF16)
-        for target in range(send_ref.shape[0]):
-            send_ref[target] = value
+    first_copy = pltpu.make_async_copy(
+        s_hbm.at[:, pl.ds(s_hbm.shape[1] - rows_ref.shape[1], rows_ref.shape[1]), :], rows_ref, sems.at[heads]
+    )
+    first_copy.start()
+    copies = []
+    for head in range(heads):
+        span = pl.ds(head * dv, dv)
+        copies.append(pltpu.make_async_copy(w_hbm.at[span, :], w_ref.at[span, :], sems.at[head]))
+        copies[-1].start()
+    first_copy.wait()
+    total = rows_ref[0, :own].astype(F32)
+    for member in range(1, GROUP):
+        total = total + rows_ref[member, :own].astype(F32)
+    lines[...] = total
+    tails = [rows_ref[member, own:].astype(F32) for member in range(GROUP)]
+    gated = []
+    for head in range(heads):
+        both = tails[2 * head][REQ : 2 * REQ] + tails[2 * head + 1][REQ : 2 * REQ]
+        scale = lax.rsqrt(jnp.sum(both, axis=1, keepdims=True) / dv + EPS)
+        halves = []
+        for member in (2 * head, 2 * head + 1):
+            halves.append(tails[member][:REQ] * scale * lines[member * REQ : (member + 1) * REQ, :])
+        gated.append(jnp.concatenate(halves, axis=1).astype(BF16))
+    mixed = None
+    for head in range(heads):
+        copies[head].wait()
+        value = dot(gated[head], w_ref[head * dv : (head + 1) * dv, :])
+        mixed = value if mixed is None else mixed + value
+    sums[...] = mixed
+    for place in range(share // dk):
+        at = pl.multiple_of(meta_ref[REQ + 1] * share + place * dk, dk)
+        first = (GROUP + place) * REQ
+        sums[:, pl.ds(at, dk)] += lines[first : first + REQ, :]
+    value = sums[...].astype(BF16)
+    for target in range(send_ref.shape[0]):
+        send_ref[target] = value
 
 
 def head_kernel(lasts_ref, gain_ref, w_ref, out_ref):
@@ -500,30 +515,18 @@
 
     halo = lax.ppermute(states_in[tok - HALO :], "seq", [(i, i + 1) for i in range(seq_count - 1)])
     gain = attn_gain[None, :]
-    normed, scal = pl.pallas_call(
-        norm_kernel,
-        out_shape=(shape((tok, model), BF16), shape((tok, 128), F32)),
-        grid=(1,),
-        in_specs=[
-            whole(tok, model), whole(1, model), whole(heads, model), whole(heads, model), whole(1, heads),
-            whole(1, heads),
-        ],
-        out_specs=(whole(tok, model), whole(tok, 128)),
-        compiler_params=params(24),
-        name="norm_kernel",
-    )(*hbm(states_in, gain, w_beta.T, w_alpha.T, decay_rate[None, :], decay_bias[None, :]))
-
-    maps, qa, own, a_all, b_all = pl.pallas_call(
+    maps, normed, qa, own, a_all, b_all = pl.pallas_call(
         maps_kernel,
         out_shape=(
             shape((2 * heads, 2 * dk + 2 * PAD, dk), BF16),
+            pltpu.HBM((tok, model), BF16),
             pltpu.HBM((blocks, heads, BLOCK_LEN, dk), BF16),
             pltpu.HBM((blocks, heads, BLOCK_LEN, dv), F32),
             pltpu.HBM((blocks, heads, dk, dk), F32),
             pltpu.HBM((blocks, heads, dk, dv), F32),
         ),
-        in_specs=[SMEM, VMEM, VMEM] + [HBM] * 7 + [VMEM],
-        out_specs=(VMEM, HBM, HBM, HBM, HBM),
+        in_specs=[SMEM, VMEM] + [HBM] * 12,
+        out_specs=(VMEM,) + (HBM,) * 5,
         scratch_shapes=[
             pltpu.VMEM((HALO + tok, model), BF16),
             pltpu.VMEM((HALO + tok, 2 * heads * dk + heads * dv), F32),
@@ -535,18 +538,32 @@
             pltpu.VMEM((blocks, heads, dk, dk), F32),
             pltpu.VMEM((blocks, heads, dk, dv), F32),
             pltpu.SemaphoreType.DMA((4, blocks)),
+            pltpu.VMEM((tok, 128), F32),
+            pltpu.VMEM((tok, model), BF16),
             pltpu.VMEM((1, model), F32),
+            pltpu.VMEM((heads, model), BF16),
+            pltpu.VMEM((heads, model), BF16),
+            pltpu.VMEM((1, heads), F32),
+            pltpu.VMEM((1, heads), F32),
             pltpu.VMEM(w_query.shape, BF16),
             pltpu.VMEM(w_key.shape, BF16),
             pltpu.VMEM(w_value.shape, BF16),
             pltpu.VMEM(conv_query.shape, F32),
             pltpu.VMEM(conv_key.shape, F32),
             pltpu.VMEM(conv_value.shape, F32),
-            pltpu.SemaphoreType.DMA((7,)),
+            pltpu.SemaphoreType.DMA((12,)),
+            pltpu.SemaphoreType.DMA((1,)),
         ],
         compiler_params=params(40),
         name="maps_kernel",
-    )(meta, normed, halo, *hbm(gain, w_query, w_key, w_value, conv_query, conv_key, conv_value), scal)
+    )(
+        meta,
+        halo,
+        *hbm(
+            states_in, gain, w_beta.T, w_alpha.T, decay_rate[None, :], decay_bias[None, :], w_query, w_key, w_value,
+            conv_query, conv_key, conv_value,
+        ),
+    )
 
     got = group_exchange(maps)
     gate, own_rows = pl.pallas_call(
@@ -597,20 +614,15 @@
     sends = pl.pallas_call(
         rows_kernel,
         out_shape=shape((groups * tp_count, REQ, model), BF16),
-        grid_spec=pltpu.PrefetchScalarGridSpec(
-            num_scalar_prefetch=1,
-            grid=(heads,),
-            in_specs=[
-                pl.BlockSpec((GROUP, rows_len, dk), lambda i, m: (0, dk // rows_len, 0)),
-                pl.BlockSpec((dv, model), lambda i, m: (i, 0)),
-            ],
-            out_specs=whole(groups * tp_count, REQ, model),
-            scratch_shapes=[
-                pltpu.VMEM((heads, REQ, dv), BF16),
-                pltpu.VMEM((REQ, model), F32),
-                pltpu.VMEM((rows_len - PAD, dk), F32),
-            ],
-        ),
+        in_specs=[SMEM, HBM, HBM],
+        out_specs=VMEM,
+        scratch_shapes=[
+            pltpu.VMEM((GROUP, rows_len, dk), BF16),
+            pltpu.VMEM(w_out.shape, BF16),
+            pltpu.VMEM((REQ, model), F32),
+            pltpu.VMEM((rows_len - PAD, dk), F32),
+            pltpu.SemaphoreType.DMA((heads + 1,)),
+        ],
         compiler_params=params(24),
         name="rows_kernel",
     )(meta, *hbm(s_in, w_out))

time: 114 us -> 113 us (level)
  Pallas kernels: 41.6 us -> 38.3 us
  starting transfers between devices: 30.6 us -> 33.1 us
    pallas_call x1 -> x0, Pallas kernels: 2.99 us -> none  [body(): pl.pallas_call(norm_kernel, out_shape=(shape((tok, model), BF16), shape((...]
    all_to_all x1, starting transfers between devices: 4.3 us -> 5.65 us  [group_exchange(): return lax.all_to_all(value, 'seq', 0, 0, axis_index_groups=groups)]
  transfers between devices with their start and end apart: 8 -> 8, of which waited for: 3 -> 4; matrix products, arithmetic and copies ran while one was open for 1% -> 1% of each run, Pallas kernels for 12% -> 10%
where the time goes in v1:
time: 113 us
  Pallas kernels  38.3 us (34%)
  starting transfers between devices  33.1 us (29%)
  blocking collectives  26.8 us (24%)
  waiting for transfers between devices  10.6 us (9%)
  other arithmetic  2.23 us (2%)
    pallas_call x1, Pallas kernels, body(): pl.pallas_call(maps_kernel, out_shape=(shape((2 * heads, 2 * dk + 2 * PAD...  15.3 us
    all_to_all x1, blocking collectives, body(): lasts = lax.all_to_all(sends, ('seq', 'tp'), 0, 0, axis_index_groups=joint)  13.6 us
    all_to_all x1, blocking collectives, group_exchange(): return lax.all_to_all(value, 'seq', 0, 0, axis_index_groups=groups)  13.2 us
    ppermute x2, starting transfers between devices, shift_groups(): lax.ppermute(value, 'seq', [(source, source + gap) for source in range(co...  8.78 us
    all_to_all x1, starting transfers between devices, body(): bests = lax.all_to_all(spread, ('seq', 'tp'), 0, 0)  8.33 us
    ppermute x3, starting transfers between devices, body(): mixed = mixed + lax.ppermute(value, 'tp', ring).astype(F32)  5.73 us
    all_to_all x1, starting transfers between devices, group_exchange(): return lax.all_to_all(value, 'seq', 0, 0, axis_index_groups=groups)  5.65 us
    pallas_call x1, Pallas kernels, body(): pl.pallas_call(gate_kernel, out_shape=(shape((tok, heads * dv), F32), sha...  5.11 us
  transfers between devices with their start and end apart: 8, of which 4 were waited for; matrix products, arithmetic and copies ran while one was open for 1% of the time, Pallas kernels for 10%

profile of v1, /device:TPU:1, one launch (start us, length us, event | category | flops | bytes accessed | tf_op | source)
XLA Modules:
  0.0 112.6 jit_solution(2500742910932712401)
XLA Ops:
  0.6 0.8 slice.9
  1.5 4.6 %collective-permute-start = (bf16[16,2048]{1,0:T(8,128)(2,1)S(1)}, bf16[16,2048]{1,0:T(8,128)(2,1)S(1)}, u32[]{:S(2)}, u32[]{:S(2)}) collective-permute-start(bf16[16,2048]{1,0:T(8,128)(2,1)S(1)} %slice.9), channel_id=1, source_target_pairs={{0,4},{4,8},{8,12},{12,16},{16,20},{20,24},{24,28},{28,32},{32,36}... | collective-permute-start | bytes 196616 | tf_op jit(solution)/shard_map/ppermute | solution.py:516
  6.1 0.7 pad_add_fusion.meta_ref
  6.8 0.6 collective-permute-done.halo_ref
  7.4 15.3 %maps_kernel.1 = (bf16[8,288,128]{2,1,0:T(8,128)(2,1)}, bf16[256,2048]{1,0:T(8,128)(2,1)}, bf16[4,4,64,128]{3,2,1,0:T(8,128)(2,1)}, f32[4,4,64,256]{3,2,1,0:T(8,...) custom-call(s32[6]{0:T(128)S(1)} %pad_add_fusion.meta_ref, ...), custom_call_target="tpu_custom_call" | custom-call | tf_op jit(solution)/shard_map/maps_kernel/pallas_call | solution.py:518
  22.7 5.7 %all-to-all-start = ((bf16[8,288,128]{2,1,0:T(8,128)(2,1)}), bf16[8,288,128]{2,1,0:T(8,128)(2,1)S(1)}, u32[]{:S(2)}, u32[]{:S(2)}) async-start(bf16[8,288,128]{2,1,0:T(8,128)(2,1)} %get-tuple-element.24), calls=%async_computation | async-start | bytes 1179648 | tf_op jit(solution)/shard_map/all_to_all | solution.py:45
  28.3 0.0 copy-start.5
  28.3 5.1 %gate_kernel.1 = (f32[256,1024]{1,0:T(8,128)S(1)}, bf16[48,128]{1,0:T(8,128)(2,1)S(1)}) custom-call(s32[6]{0:T(128)S(1)} %pad_add_fusion.meta_ref, bf16[256,2048]{1,0:T(8,128)(2,1)} %get-tuple-element.25.normed_ref, bf16[2048,1024]{1,0:T(8,128)(2,1)} %w_gate_ref.1, bf16[256,2048]{1,0:T(8,128)(2,1)} %x_ref.3), custom_call_target="tpu_custom_call" | custom-call | tf_op jit(solution)/shard_map/gate_kernel/pallas_call | solution.py:569
  33.4 4.9 %all-to-all-done.got_ref = bf16[8,288,128]{2,1,0:T(8,128)(2,1)S(1)} async-done(((bf16[8,288,128]{2,1,0:T(8,128)(2,1)}), bf16[8,288,128]{2,1,0:T(8,128)(2,1)S(1)}, u32[]{:S(2)}, u32[]{:S(2)}) %all-to-all-start) | async-done | bytes 589856 | tf_op jit(solution)/shard_map/all_to_all | solution.py:45
  38.4 1.5 %scan_kernel.1 = (f32[8,128,256]{2,1,0:T(8,128)S(1)}, bf16[1,272,128]{2,1,0:T(8,128)(2,1)S(1)}) custom-call(bf16[8,288,128]{2,1,0:T(8,128)(2,1)S(1)} %all-to-all-done.got_ref), custom_call_target="tpu_custom_call" | custom-call | tf_op jit(solution)/shard_map/scan_kernel/pallas_call | solution.py:587
  39.9 4.2 %collective-permute-start.1 = (bf16[1,272,128]{2,1,0:T(8,128)(2,1)S(1)}, bf16[1,272,128]{2,1,0:T(8,128)(2,1)S(1)}, u32[]{:S(2)}, u32[]{:S(2)}) collective-permute-start(bf16[1,272,128]{2,1,0:T(8,128)(2,1)S(1)} %get-tuple-element.29), channel_id=1, source_target_pairs={{0,32},{4,36},{8,40},{12,44},{16,48},{20,52},{24,56},{28,60},{32,6... | collective-permute-start | bytes 208904 | tf_op jit(solution)/shard_map/ppermute | solution.py:39
  44.2 4.5 %collective-permute-start.2 = (bf16[128,128]{1,0:T(8,128)(2,1)S(1)}, bf16[128,128]{1,0:T(8,128)(2,1)S(1)}, u32[]{:S(2)}, u32[]{:S(2)}) collective-permute-start(bf16[128,128]{1,0:T(8,128)(2,1)S(1)} %slice_bitcast_fusion), channel_id=1, source_target_pairs={{0,64},{4,68},{8,72},{12,76},{16,80},{20,84},{24,88},{28,92},{32,9... | collective-permute-start | bytes 98312 | tf_op jit(solution)/shard_map/ppermute | solution.py:39
  48.7 0.8 collective-permute-done.2.two_ref
  49.5 0.0 collective-permute-done.1.one_ref
  49.5 0.0 copy-done.5
  49.5 2.4 %apply_kernel.1 = bf16[8,192,128]{2,1,0:T(8,128)(2,1)S(1)} custom-call(s32[6]{0:T(128)S(1)} %pad_add_fusion.meta_ref, bf16[1,272,128]{2,1,0:T(8,128)(2,1)S(1)} %collective-permute-done.1.one_ref, bf16[128,128]{1,0:T(8,128)(2,1)S(1)} %collective-permute-done.2.two_ref, f32[8,128,256]{2,1,0:T(8,128)S(1)} %get-tuple-element.30.before_ref, ...), custom_call_target="tpu_custom_call" | custom-call | tf_op jit(solution)/shard_map/apply_kernel/pallas_call | solution.py:598
  51.9 13.2 %all_to_all.20.s_hbm.s_ref = bf16[8,192,128]{2,1,0:T(8,128)(2,1)} all-to-all(bf16[8,192,128]{2,1,0:T(8,128)(2,1)S(1)} %apply_kernel.1), channel_id=1, replica_groups={{0,4,8,12,16,20,24,28},{32,36,40,44,48,52,56,60},{64,68,72,76,80,84,88,..., dimensions={0} | all-to-all | bytes 786432 | tf_op jit(solution)/shard_map/all_to_all | solution.py:45
  65.1 0.0 copy-start
  65.1 0.0 copy-start.2
  65.1 0.0 copy-start.3
  65.1 3.1 %rows_kernel.1 = bf16[16,4,2048]{2,1,0:T(4,128)(2,1)S(1)} custom-call(s32[6]{0:T(128)S(1)} %pad_add_fusion.meta_ref, bf16[8,192,128]{2,1,0:T(8,128)(2,1)} %all_to_all.20.s_hbm.s_ref, bf16[1024,2048]{1,0:T(8,128)(2,1)} %w_ref.2), custom_call_target="tpu_custom_call" | custom-call | tf_op jit(solution)/shard_map/rows_kernel/pallas_call | solution.py:614
  68.3 0.0 copy-done
  68.3 0.0 copy-done.2
  68.3 0.0 copy-done.3
  68.3 0.5 output_kernel.1.gated_ref
  68.8 0.0 copy-start.1
  68.8 0.0 copy-start.4
  68.8 4.6 %mix_kernel.1 = (bf16[256,512]{1,0:T(8,128)(2,1)S(1)}, bf16[256,512]{1,0:T(8,128)(2,1)S(1)}, bf16[256,512]{1,0:T(8,128)(2,1)S(1)}, f32[256,512]{1,0:T(8,128)S(1)}) custom-call(s32[6]{0:T(128)S(1)} %pad_add_fusion.meta_ref, bf16[256,1024]{1,0:T(8,128)(2,1)S(1)} %output_kernel.1.gated_ref, bf16[1024,2048]{1,0:T(8,128)(2,1)} %w_ref.2, bf16[256,2048]{1,0:T(8,128)(2,1)} %x_ref.3), custom_call_target="tpu_custom_call" | custom-call | tf_op jit(solution)/shard_map/mix_kernel/pallas_call | solution.py:648
  73.4 1.7 %collective-permute-start.3 = (bf16[256,512]{1,0:T(8,128)(2,1)S(1)}, bf16[256,512]{1,0:T(8,128)(2,1)S(1)}, u32[]{:S(2)}, u32[]{:S(2)}) collective-permute-start(bf16[256,512]{1,0:T(8,128)(2,1)S(1)} %get-tuple-element.37), channel_id=1, source_target_pairs={{0,1},{1,2},{2,3},{3,0},{4,5},{5,6},{6,7},{7,4},{8,9},{9,10},{10,1... | collective-permute-start | bytes 786440 | tf_op jit(solution)/shard_map/ppermute | solution.py:693
  75.1 3.3 %collective-permute-start.4 = (bf16[256,512]{1,0:T(8,128)(2,1)S(1)}, bf16[256,512]{1,0:T(8,128)(2,1)S(1)}, u32[]{:S(2)}, u32[]{:S(2)}) collective-permute-start(bf16[256,512]{1,0:T(8,128)(2,1)S(1)} %get-tuple-element.38), channel_id=1, source_target_pairs={{0,2},{1,3},{2,0},{3,1},{4,6},{5,7},{6,4},{7,5},{8,10},{9,11},{10,... | collective-permute-start | bytes 786440 | tf_op jit(solution)/shard_map/ppermute | solution.py:693
  78.4 0.7 collective-permute-start.5
  79.2 13.6 %all_to_all.21.lasts_ref = bf16[16,4,2048]{2,1,0:T(4,128)(2,1)S(1)} all-to-all(bf16[16,4,2048]{2,1,0:T(4,128)(2,1)S(1)} %rows_kernel.1), channel_id=1, replica_groups={{0,1,2,3,32,33,34,35,64,65,66,67,96,97,98,99},{4,5,6,7,36,37,38,39,68,6..., dimensions={0} | all-to-all | bytes 524288 | tf_op jit(solution)/shard_map/all_to_all | solution.py:630
  92.7 0.0 copy-done.1
  92.7 0.0 copy-done.4
  92.7 1.2 %head_kernel.1 = f32[128,1,128]{2,1,0:T(1,128)} custom-call(bf16[16,4,2048]{2,1,0:T(4,128)(2,1)S(1)} %all_to_all.21.lasts_ref, f32[1,2048]{1,0:T(1,128)S(1)} %bitcast.11, bf16[2048,250]{1,0:T(8,128)(2,1)S(1)} %copy-done.1), custom_call_target="tpu_custom_call" | custom-call | tf_op jit(solution)/shard_map/head_kernel/pallas_call | solution.py:666
  93.9 8.3 %all-to-all-start.3 = ((f32[128,1,128]{2,1,0:T(1,128)}), f32[128,1,128]{2,1,0:T(1,128)S(1)}, u32[]{:S(2)}, u32[]{:S(2)}) async-start(f32[128,1,128]{2,1,0:T(1,128)} %head_kernel.1), calls=%async_computation.3 | async-start | bytes 131072 | tf_op jit(solution)/shard_map/all_to_all | solution.py:676
  102.3 4.5 %states_kernel.1 = f32[4,4,128,256]{3,2,1,0:T(8,128)} custom-call(f32[4,4,128,128]{3,2,1,0:T(8,128)} %get-tuple-element.40.a_ref, f32[4,4,128,256]{3,2,1,0:T(8,128)} %get-tuple-element.41.b_ref, bf16[8,192,128]{2,1,0:T(8,128)(2,1)} %all_to_all.20.s_hbm.s_ref), custom_call_target="tpu_custom_call" | custom-call | tf_op jit(solution)/shard_map/states_kernel/pallas_call | solution.py:677
  106.8 0.0 collective-permute-done.3
  106.8 0.0 collective-permute-done.4
  106.8 0.0 collective-permute-done.5
  106.8 0.8 add_convert_fusion
  107.7 4.3 %all-to-all-done.3 = f32[128,1,128]{2,1,0:T(1,128)S(1)} async-done(((f32[128,1,128]{2,1,0:T(1,128)}), f32[128,1,128]{2,1,0:T(1,128)S(1)}, u32[]{:S(2)}, u32[]{:S(2)}) %all-to-all-start.3) | async-done | bytes 65568 | tf_op jit(solution)/shard_map/all_to_all | solution.py:676
  112.0 0.7 slice_reduce_fusion
  (1 shorter events, 0.0 us)
Async XLA Ops:
  1.5 5.9 %collective-permute-start = (bf16[16,2048]{1,0:T(8,128)(2,1)S(1)}, bf16[16,2048]{1,0:T(8,128)(2,1)S(1)}, u32[]{:S(2)}, u32[]{:S(2)}) collective-permute-start(bf16[16,2048]{1,0:T(8,128)(2,1)S(1)} %slice.9), channel_id=1, source_target_pairs={{0,4},{4,8},{8,12},{12,16},{16,20},{20,24},{24,28},{28,32},{32,36}... | collective-permute-start | bytes 196616 | tf_op jit(solution)/shard_map/ppermute | solution.py:516
  22.7 15.7 %all-to-all-start = ((bf16[8,288,128]{2,1,0:T(8,128)(2,1)}), bf16[8,288,128]{2,1,0:T(8,128)(2,1)S(1)}, u32[]{:S(2)}, u32[]{:S(2)}) async-start(bf16[8,288,128]{2,1,0:T(8,128)(2,1)} %get-tuple-element.24), calls=%async_computation | async-start | bytes 1179648 | tf_op jit(solution)/shard_map/all_to_all | solution.py:45
  28.3 21.2 %copy-start.5 = (f32[256]{0:T(256)S(1)}, f32[256]{0:T(256)}, u32[]{:S(2)}) copy-start(f32[256]{0:T(256)} %param.32) | copy-start | bytes 3076
  39.9 9.6 %collective-permute-start.1 = (bf16[1,272,128]{2,1,0:T(8,128)(2,1)S(1)}, bf16[1,272,128]{2,1,0:T(8,128)(2,1)S(1)}, u32[]{:S(2)}, u32[]{:S(2)}) collective-permute-start(bf16[1,272,128]{2,1,0:T(8,128)(2,1)S(1)} %get-tuple-element.29), channel_id=1, source_target_pairs={{0,32},{4,36},{8,40},{12,44},{16,48},{20,52},{24,56},{28,60},{32,6... | collective-permute-start | bytes 208904 | tf_op jit(solution)/shard_map/ppermute | solution.py:39
  44.2 5.4 %collective-permute-start.2 = (bf16[128,128]{1,0:T(8,128)(2,1)S(1)}, bf16[128,128]{1,0:T(8,128)(2,1)S(1)}, u32[]{:S(2)}, u32[]{:S(2)}) collective-permute-start(bf16[128,128]{1,0:T(8,128)(2,1)S(1)} %slice_bitcast_fusion), channel_id=1, source_target_pairs={{0,64},{4,68},{8,72},{12,76},{16,80},{20,84},{24,88},{28,92},{32,9... | collective-permute-start | bytes 98312 | tf_op jit(solution)/shard_map/ppermute | solution.py:39
  65.1 3.1 %copy-start = (bf16[8,192,128]{2,1,0:T(8,128)(2,1)S(1)}, bf16[8,192,128]{2,1,0:T(8,128)(2,1)}, u32[]{:S(2)}) copy-start(bf16[8,192,128]{2,1,0:T(8,128)(2,1)} %all_to_all.20.s_hbm.s_ref) | copy-start | bytes 1179652
  65.1 3.1 %copy-start.2 = (f32[4,4,64,256]{3,2,1,0:T(8,128)S(1)}, f32[4,4,64,256]{3,2,1,0:T(8,128)}, u32[]{:S(2)}) copy-start(f32[4,4,64,256]{3,2,1,0:T(8,128)} %get-tuple-element.34.own_ref) | copy-start | bytes 3145732
  65.1 3.2 %copy-start.3 = (bf16[4,4,64,128]{3,2,1,0:T(8,128)(2,1)S(1)}, bf16[4,4,64,128]{3,2,1,0:T(8,128)(2,1)}, u32[]{:S(2)}) copy-start(bf16[4,4,64,128]{3,2,1,0:T(8,128)(2,1)} %get-tuple-element.33.qa_ref) | copy-start | bytes 786436
  68.8 24.0 %copy-start.1 = (bf16[2048,250]{1,0:T(8,128)(2,1)S(1)}, bf16[2048,250]{1,0:T(8,128)(2,1)}, u32[]{:S(2)}) copy-start(bf16[2048,250]{1,0:T(8,128)(2,1)} %w_ref.3) | copy-start | bytes 3072004
  68.8 24.0 %copy-start.4 = (f32[2048]{0:T(1024)S(1)}, f32[2048]{0:T(1024)}, u32[]{:S(2)}) copy-start(f32[2048]{0:T(1024)} %param.34) | copy-start | bytes 24580
  73.4 33.4 %collective-permute-start.3 = (bf16[256,512]{1,0:T(8,128)(2,1)S(1)}, bf16[256,512]{1,0:T(8,128)(2,1)S(1)}, u32[]{:S(2)}, u32[]{:S(2)}) collective-permute-start(bf16[256,512]{1,0:T(8,128)(2,1)S(1)} %get-tuple-element.37), channel_id=1, source_target_pairs={{0,1},{1,2},{2,3},{3,0},{4,5},{5,6},{6,7},{7,4},{8,9},{9,10},{10,1... | collective-permute-start | bytes 786440 | tf_op jit(solution)/shard_map/ppermute | solution.py:693
  75.1 31.7 %collective-permute-start.4 = (bf16[256,512]{1,0:T(8,128)(2,1)S(1)}, bf16[256,512]{1,0:T(8,128)(2,1)S(1)}, u32[]{:S(2)}, u32[]{:S(2)}) collective-permute-start(bf16[256,512]{1,0:T(8,128)(2,1)S(1)} %get-tuple-element.38), channel_id=1, source_target_pairs={{0,2},{1,3},{2,0},{3,1},{4,6},{5,7},{6,4},{7,5},{8,10},{9,11},{10,... | collective-permute-start | bytes 786440 | tf_op jit(solution)/shard_map/ppermute | solution.py:693
  78.4 28.4 %collective-permute-start.5 = (bf16[256,512]{1,0:T(8,128)(2,1)S(1)}, bf16[256,512]{1,0:T(8,128)(2,1)S(1)}, u32[]{:S(2)}, u32[]{:S(2)}) collective-permute-start(bf16[256,512]{1,0:T(8,128)(2,1)S(1)} %get-tuple-element.39), channel_id=1, source_target_pairs={{0,3},{1,0},{2,1},{3,2},{4,7},{5,4},{6,5},{7,6},{8,11},{9,8},{10,9... | collective-permute-start | bytes 786440 | tf_op jit(solution)/shard_map/ppermute | solution.py:693
  93.9 18.0 %all-to-all-start.3 = ((f32[128,1,128]{2,1,0:T(1,128)}), f32[128,1,128]{2,1,0:T(1,128)S(1)}, u32[]{:S(2)}, u32[]{:S(2)}) async-start(f32[128,1,128]{2,1,0:T(1,128)} %head_kernel.1), calls=%async_computation.3 | async-start | bytes 131072 | tf_op jit(solution)/shard_map/all_to_all | solution.py:676

commit v2 on v1

--- a/solution.py
+++ b/solution.py
@@ -36,7 +36,7 @@
 def shift_groups(value, steps):
     count = lax.axis_size("seq")
     gap = steps * GROUP
-    return lax.ppermute(value, "seq", [(source, source + gap) for source in range(count - gap)])
+    return lax.ppermute(value, "seq", [(source, (source + gap) % count) for source in range(count)])
 
 
 def group_exchange(value):
@@ -374,10 +374,10 @@
     eye = rows == cols
     a, b = load_map(one_ref[0], eye)
     a_high, a_low = split(a)
-    entering = dot(a_high, two_ref[...]) + dot(a_low, two_ref[...]) + b
-    e_high, e_low = split(entering)
     part = meta_ref[REQ] % 2
     group = meta_ref[REQ] // GROUP
+    entering = jnp.where(group >= 2, dot(a_high, two_ref[...]) + dot(a_low, two_ref[...]), 0.0) + b
+    e_high, e_low = split(jnp.where(group >= 1, entering, 0.0))
     gain = jnp.where(part == 0, gain_ref[:, :size], gain_ref[:, size:])
     final = last_blocks(meta_ref)
     kept = [jnp.zeros((REQ, size), F32), jnp.zeros((REQ, 1), F32)]
@@ -513,7 +513,7 @@
     params = lambda mib: pltpu.CompilerParams(vmem_limit_bytes=mib << 20)
     meta = jnp.concatenate([lengths, piece[None], shard[None]]).astype(jnp.int32)
 
-    halo = lax.ppermute(states_in[tok - HALO :], "seq", [(i, i + 1) for i in range(seq_count - 1)])
+    halo = lax.ppermute(states_in[tok - HALO :], "seq", [(i, (i + 1) % seq_count) for i in range(seq_count)])
     gain = attn_gain[None, :]
     maps, normed, qa, own, a_all, b_all = pl.pallas_call(
         maps_kernel,

time: 113 us -> 108 us (0.956)
  starting transfers between devices: 33.1 us -> 25.6 us
  waiting for transfers between devices: 10.6 us -> 12 us
    ppermute x3, starting transfers between devices: 13.3 us -> 5.48 us  [the longest x2 2.81 us: shift_groups(): lax.ppermute(value, 'seq', [(source, (source + gap) % count) for source i...]
    all_to_all x1, starting transfers between devices: 5.65 us -> 7.84 us  [group_exchange(): return lax.all_to_all(value, 'seq', 0, 0, axis_index_groups=groups)]
    all_to_all x1, starting transfers between devices: 8.33 us -> 6.42 us  [body(): bests = lax.all_to_all(spread, ('seq', 'tp'), 0, 0)]
    ppermute x3, waiting for transfers between devices: 1.4 us -> 2.76 us  [the longest x2 2.16 us: shift_groups(): lax.ppermute(value, 'seq', [(source, (source + gap) % count) for source i...]
where the time goes in v2:
time: 108 us; the launch traced here: 107 us
  Pallas kernels  38.3 us (35%)
  blocking collectives  27.7 us (26%)
  starting transfers between devices  25.6 us (24%)
  waiting for transfers between devices  12 us (11%)
  other arithmetic  2.23 us (2%)
    pallas_call x1, Pallas kernels, body(): pl.pallas_call(maps_kernel, out_shape=(shape((2 * heads, 2 * dk + 2 * PAD...  15.3 us
    all_to_all x1, blocking collectives, body(): lasts = lax.all_to_all(sends, ('seq', 'tp'), 0, 0, axis_index_groups=joint)  14.5 us
    all_to_all x1, blocking collectives, group_exchange(): return lax.all_to_all(value, 'seq', 0, 0, axis_index_groups=groups)  13.2 us
    all_to_all x1, starting transfers between devices, group_exchange(): return lax.all_to_all(value, 'seq', 0, 0, axis_index_groups=groups)  7.84 us
    all_to_all x1, starting transfers between devices, body(): bests = lax.all_to_all(spread, ('seq', 'tp'), 0, 0)  6.42 us
    ppermute x3, starting transfers between devices, body(): mixed = mixed + lax.ppermute(value, 'tp', ring).astype(F32)  5.85 us
    pallas_call x1, Pallas kernels, body(): pl.pallas_call(gate_kernel, out_shape=(shape((tok, heads * dv), F32), sha...  5.11 us
    all_to_all x1, waiting for transfers between devices, group_exchange(): return lax.all_to_all(value, 'seq', 0, 0, axis_index_groups=groups)  4.96 us
  transfers between devices with their start and end apart: 8, of which 4 were waited for; matrix products, arithmetic and copies ran while one was open for 1% of the time, Pallas kernels for 10%

profile of v2, /device:TPU:1, one launch (start us, length us, event | category | flops | bytes accessed | tf_op | source)
XLA Modules:
  0.0 107.4 jit_solution(588226810131369358)
XLA Ops:
  0.6 0.8 slice.9
  1.5 2.7 %collective-permute-start = (bf16[16,2048]{1,0:T(8,128)(2,1)S(1)}, bf16[16,2048]{1,0:T(8,128)(2,1)S(1)}, u32[]{:S(2)}, u32[]{:S(2)}) collective-permute-start(bf16[16,2048]{1,0:T(8,128)(2,1)S(1)} %slice.9), channel_id=1, source_target_pairs={{0,4},{4,8},{8,12},{12,16},{16,20},{20,24},{24,28},{28,32},{32,36}... | collective-permute-start | bytes 196616 | tf_op jit(solution)/shard_map/ppermute | solution.py:516
  4.2 0.7 pad_add_fusion.meta_ref
  4.9 0.6 collective-permute-done.halo_ref
  5.5 15.3 %maps_kernel.1 = (bf16[8,288,128]{2,1,0:T(8,128)(2,1)}, bf16[256,2048]{1,0:T(8,128)(2,1)}, bf16[4,4,64,128]{3,2,1,0:T(8,128)(2,1)}, f32[4,4,64,256]{3,2,1,0:T(8,...) custom-call(s32[6]{0:T(128)S(1)} %pad_add_fusion.meta_ref, ...), custom_call_target="tpu_custom_call" | custom-call | tf_op jit(solution)/shard_map/maps_kernel/pallas_call | solution.py:518
  20.8 7.8 %all-to-all-start = ((bf16[8,288,128]{2,1,0:T(8,128)(2,1)}), bf16[8,288,128]{2,1,0:T(8,128)(2,1)S(1)}, u32[]{:S(2)}, u32[]{:S(2)}) async-start(bf16[8,288,128]{2,1,0:T(8,128)(2,1)} %get-tuple-element.24), calls=%async_computation | async-start | bytes 1179648 | tf_op jit(solution)/shard_map/all_to_all | solution.py:45
  28.6 0.0 copy-start.5
  28.6 5.1 %gate_kernel.1 = (f32[256,1024]{1,0:T(8,128)S(1)}, bf16[48,128]{1,0:T(8,128)(2,1)S(1)}) custom-call(s32[6]{0:T(128)S(1)} %pad_add_fusion.meta_ref, bf16[256,2048]{1,0:T(8,128)(2,1)} %get-tuple-element.25.normed_ref, bf16[2048,1024]{1,0:T(8,128)(2,1)} %w_gate_ref.1, bf16[256,2048]{1,0:T(8,128)(2,1)} %x_ref.3), custom_call_target="tpu_custom_call" | custom-call | tf_op jit(solution)/shard_map/gate_kernel/pallas_call | solution.py:569
  33.7 5.0 %all-to-all-done.got_ref = bf16[8,288,128]{2,1,0:T(8,128)(2,1)S(1)} async-done(((bf16[8,288,128]{2,1,0:T(8,128)(2,1)}), bf16[8,288,128]{2,1,0:T(8,128)(2,1)S(1)}, u32[]{:S(2)}, u32[]{:S(2)}) %all-to-all-start) | async-done | bytes 589856 | tf_op jit(solution)/shard_map/all_to_all | solution.py:45
  38.7 1.5 %scan_kernel.1 = (f32[8,128,256]{2,1,0:T(8,128)S(1)}, bf16[1,272,128]{2,1,0:T(8,128)(2,1)S(1)}) custom-call(bf16[8,288,128]{2,1,0:T(8,128)(2,1)S(1)} %all-to-all-done.got_ref), custom_call_target="tpu_custom_call" | custom-call | tf_op jit(solution)/shard_map/scan_kernel/pallas_call | solution.py:587
  40.2 0.4 collective-permute-start.1
  40.6 2.4 %collective-permute-start.2 = (bf16[128,128]{1,0:T(8,128)(2,1)S(1)}, bf16[128,128]{1,0:T(8,128)(2,1)S(1)}, u32[]{:S(2)}, u32[]{:S(2)}) collective-permute-start(bf16[128,128]{1,0:T(8,128)(2,1)S(1)} %slice_bitcast_fusion), channel_id=1, source_target_pairs={{0,64},{4,68},{8,72},{12,76},{16,80},{20,84},{24,88},{28,92},{32,9... | collective-permute-start | bytes 98312 | tf_op jit(solution)/shard_map/ppermute | solution.py:39
  43.1 2.1 %collective-permute-done.2.two_ref = bf16[128,128]{1,0:T(8,128)(2,1)S(1)} collective-permute-done((bf16[128,128]{1,0:T(8,128)(2,1)S(1)}, bf16[128,128]{1,0:T(8,128)(2,1)S(1)}, u32[]{:S(2)}, u32[]{:S(2)}) %collective-permute-start.2) | collective-permute-done | bytes 32800 | tf_op jit(solution)/shard_map/ppermute | solution.py:39
  45.2 0.0 collective-permute-done.1.one_ref
  45.2 0.0 copy-done.5
  45.2 2.4 %apply_kernel.1 = bf16[8,192,128]{2,1,0:T(8,128)(2,1)S(1)} custom-call(s32[6]{0:T(128)S(1)} %pad_add_fusion.meta_ref, bf16[1,272,128]{2,1,0:T(8,128)(2,1)S(1)} %collective-permute-done.1.one_ref, bf16[128,128]{1,0:T(8,128)(2,1)S(1)} %collective-permute-done.2.two_ref, f32[8,128,256]{2,1,0:T(8,128)S(1)} %get-tuple-element.30.before_ref, ...), custom_call_target="tpu_custom_call" | custom-call | tf_op jit(solution)/shard_map/apply_kernel/pallas_call | solution.py:598
  47.6 13.2 %all_to_all.20.s_hbm.s_ref = bf16[8,192,128]{2,1,0:T(8,128)(2,1)} all-to-all(bf16[8,192,128]{2,1,0:T(8,128)(2,1)S(1)} %apply_kernel.1), channel_id=1, replica_groups={{0,4,8,12,16,20,24,28},{32,36,40,44,48,52,56,60},{64,68,72,76,80,84,88,..., dimensions={0} | all-to-all | bytes 786432 | tf_op jit(solution)/shard_map/all_to_all | solution.py:45
  60.8 0.0 copy-start
  60.8 0.0 copy-start.2
  60.8 0.0 copy-start.3
  60.8 3.1 %rows_kernel.1 = bf16[16,4,2048]{2,1,0:T(4,128)(2,1)S(1)} custom-call(s32[6]{0:T(128)S(1)} %pad_add_fusion.meta_ref, bf16[8,192,128]{2,1,0:T(8,128)(2,1)} %all_to_all.20.s_hbm.s_ref, bf16[1024,2048]{1,0:T(8,128)(2,1)} %w_ref.2), custom_call_target="tpu_custom_call" | custom-call | tf_op jit(solution)/shard_map/rows_kernel/pallas_call | solution.py:614
  64.0 0.0 copy-done
  64.0 0.0 copy-done.2
  64.0 0.0 copy-done.3
  64.0 0.5 output_kernel.1.gated_ref
  64.5 0.0 copy-start.1
  64.5 0.0 copy-start.4
  64.5 4.6 %mix_kernel.1 = (bf16[256,512]{1,0:T(8,128)(2,1)S(1)}, bf16[256,512]{1,0:T(8,128)(2,1)S(1)}, bf16[256,512]{1,0:T(8,128)(2,1)S(1)}, f32[256,512]{1,0:T(8,128)S(1)}) custom-call(s32[6]{0:T(128)S(1)} %pad_add_fusion.meta_ref, bf16[256,1024]{1,0:T(8,128)(2,1)S(1)} %output_kernel.1.gated_ref, bf16[1024,2048]{1,0:T(8,128)(2,1)} %w_ref.2, bf16[256,2048]{1,0:T(8,128)(2,1)} %x_ref.3), custom_call_target="tpu_custom_call" | custom-call | tf_op jit(solution)/shard_map/mix_kernel/pallas_call | solution.py:648
  69.1 1.8 %collective-permute-start.3 = (bf16[256,512]{1,0:T(8,128)(2,1)S(1)}, bf16[256,512]{1,0:T(8,128)(2,1)S(1)}, u32[]{:S(2)}, u32[]{:S(2)}) collective-permute-start(bf16[256,512]{1,0:T(8,128)(2,1)S(1)} %get-tuple-element.37), channel_id=1, source_target_pairs={{0,1},{1,2},{2,3},{3,0},{4,5},{5,6},{6,7},{7,4},{8,9},{9,10},{10,1... | collective-permute-start | bytes 786440 | tf_op jit(solution)/shard_map/ppermute | solution.py:693
  70.9 3.3 %collective-permute-start.4 = (bf16[256,512]{1,0:T(8,128)(2,1)S(1)}, bf16[256,512]{1,0:T(8,128)(2,1)S(1)}, u32[]{:S(2)}, u32[]{:S(2)}) collective-permute-start(bf16[256,512]{1,0:T(8,128)(2,1)S(1)} %get-tuple-element.38), channel_id=1, source_target_pairs={{0,2},{1,3},{2,0},{3,1},{4,6},{5,7},{6,4},{7,5},{8,10},{9,11},{10,... | collective-permute-start | bytes 786440 | tf_op jit(solution)/shard_map/ppermute | solution.py:693
  74.2 0.7 collective-permute-start.5
  75.0 14.5 %all_to_all.21.lasts_ref = bf16[16,4,2048]{2,1,0:T(4,128)(2,1)S(1)} all-to-all(bf16[16,4,2048]{2,1,0:T(4,128)(2,1)S(1)} %rows_kernel.1), channel_id=1, replica_groups={{0,1,2,3,32,33,34,35,64,65,66,67,96,97,98,99},{4,5,6,7,36,37,38,39,68,6..., dimensions={0} | all-to-all | bytes 524288 | tf_op jit(solution)/shard_map/all_to_all | solution.py:630
  89.4 0.0 copy-done.1
  89.4 0.0 copy-done.4
  89.4 1.2 %head_kernel.1 = f32[128,1,128]{2,1,0:T(1,128)} custom-call(bf16[16,4,2048]{2,1,0:T(4,128)(2,1)S(1)} %all_to_all.21.lasts_ref, f32[1,2048]{1,0:T(1,128)S(1)} %bitcast.11, bf16[2048,250]{1,0:T(8,128)(2,1)S(1)} %copy-done.1), custom_call_target="tpu_custom_call" | custom-call | tf_op jit(solution)/shard_map/head_kernel/pallas_call | solution.py:666
  90.6 6.4 %all-to-all-start.3 = ((f32[128,1,128]{2,1,0:T(1,128)}), f32[128,1,128]{2,1,0:T(1,128)S(1)}, u32[]{:S(2)}, u32[]{:S(2)}) async-start(f32[128,1,128]{2,1,0:T(1,128)} %head_kernel.1), calls=%async_computation.3 | async-start | bytes 131072 | tf_op jit(solution)/shard_map/all_to_all | solution.py:676
  97.1 4.6 %states_kernel.1 = f32[4,4,128,256]{3,2,1,0:T(8,128)} custom-call(f32[4,4,128,128]{3,2,1,0:T(8,128)} %get-tuple-element.40.a_ref, f32[4,4,128,256]{3,2,1,0:T(8,128)} %get-tuple-element.41.b_ref, bf16[8,192,128]{2,1,0:T(8,128)(2,1)} %all_to_all.20.s_hbm.s_ref), custom_call_target="tpu_custom_call" | custom-call | tf_op jit(solution)/shard_map/states_kernel/pallas_call | solution.py:677
  101.6 0.0 collective-permute-done.3
  101.6 0.0 collective-permute-done.4
  101.6 0.0 collective-permute-done.5
  101.6 0.8 add_convert_fusion
  102.5 4.3 %all-to-all-done.3 = f32[128,1,128]{2,1,0:T(1,128)S(1)} async-done(((f32[128,1,128]{2,1,0:T(1,128)}), f32[128,1,128]{2,1,0:T(1,128)S(1)}, u32[]{:S(2)}, u32[]{:S(2)}) %all-to-all-start.3) | async-done | bytes 65568 | tf_op jit(solution)/shard_map/all_to_all | solution.py:676
  106.8 0.7 slice_reduce_fusion
  (1 shorter events, 0.0 us)
Async XLA Ops:
  1.5 4.0 %collective-permute-start = (bf16[16,2048]{1,0:T(8,128)(2,1)S(1)}, bf16[16,2048]{1,0:T(8,128)(2,1)S(1)}, u32[]{:S(2)}, u32[]{:S(2)}) collective-permute-start(bf16[16,2048]{1,0:T(8,128)(2,1)S(1)} %slice.9), channel_id=1, source_target_pairs={{0,4},{4,8},{8,12},{12,16},{16,20},{20,24},{24,28},{28,32},{32,36}... | collective-permute-start | bytes 196616 | tf_op jit(solution)/shard_map/ppermute | solution.py:516
  20.8 17.9 %all-to-all-start = ((bf16[8,288,128]{2,1,0:T(8,128)(2,1)}), bf16[8,288,128]{2,1,0:T(8,128)(2,1)S(1)}, u32[]{:S(2)}, u32[]{:S(2)}) async-start(bf16[8,288,128]{2,1,0:T(8,128)(2,1)} %get-tuple-element.24), calls=%async_computation | async-start | bytes 1179648 | tf_op jit(solution)/shard_map/all_to_all | solution.py:45
  28.6 16.6 %copy-start.5 = (f32[256]{0:T(256)S(1)}, f32[256]{0:T(256)}, u32[]{:S(2)}) copy-start(f32[256]{0:T(256)} %param.32) | copy-start | bytes 3076
  40.2 5.0 %collective-permute-start.1 = (bf16[1,272,128]{2,1,0:T(8,128)(2,1)S(1)}, bf16[1,272,128]{2,1,0:T(8,128)(2,1)S(1)}, u32[]{:S(2)}, u32[]{:S(2)}) collective-permute-start(bf16[1,272,128]{2,1,0:T(8,128)(2,1)S(1)} %get-tuple-element.29), channel_id=1, source_target_pairs={{0,32},{4,36},{8,40},{12,44},{16,48},{20,52},{24,56},{28,60},{32,6... | collective-permute-start | bytes 208904 | tf_op jit(solution)/shard_map/ppermute | solution.py:39
  40.6 4.6 %collective-permute-start.2 = (bf16[128,128]{1,0:T(8,128)(2,1)S(1)}, bf16[128,128]{1,0:T(8,128)(2,1)S(1)}, u32[]{:S(2)}, u32[]{:S(2)}) collective-permute-start(bf16[128,128]{1,0:T(8,128)(2,1)S(1)} %slice_bitcast_fusion), channel_id=1, source_target_pairs={{0,64},{4,68},{8,72},{12,76},{16,80},{20,84},{24,88},{28,92},{32,9... | collective-permute-start | bytes 98312 | tf_op jit(solution)/shard_map/ppermute | solution.py:39
  60.8 3.1 %copy-start = (bf16[8,192,128]{2,1,0:T(8,128)(2,1)S(1)}, bf16[8,192,128]{2,1,0:T(8,128)(2,1)}, u32[]{:S(2)}) copy-start(bf16[8,192,128]{2,1,0:T(8,128)(2,1)} %all_to_all.20.s_hbm.s_ref) | copy-start | bytes 1179652
  60.8 3.1 %copy-start.2 = (f32[4,4,64,256]{3,2,1,0:T(8,128)S(1)}, f32[4,4,64,256]{3,2,1,0:T(8,128)}, u32[]{:S(2)}) copy-start(f32[4,4,64,256]{3,2,1,0:T(8,128)} %get-tuple-element.34.own_ref) | copy-start | bytes 3145732
  60.8 3.2 %copy-start.3 = (bf16[4,4,64,128]{3,2,1,0:T(8,128)(2,1)S(1)}, bf16[4,4,64,128]{3,2,1,0:T(8,128)(2,1)}, u32[]{:S(2)}) copy-start(bf16[4,4,64,128]{3,2,1,0:T(8,128)(2,1)} %get-tuple-element.33.qa_ref) | copy-start | bytes 786436
  64.5 25.0 %copy-start.1 = (bf16[2048,250]{1,0:T(8,128)(2,1)S(1)}, bf16[2048,250]{1,0:T(8,128)(2,1)}, u32[]{:S(2)}) copy-start(bf16[2048,250]{1,0:T(8,128)(2,1)} %w_ref.3) | copy-start | bytes 3072004
  64.5 25.0 %copy-start.4 = (f32[2048]{0:T(1024)S(1)}, f32[2048]{0:T(1024)}, u32[]{:S(2)}) copy-start(f32[2048]{0:T(1024)} %param.34) | copy-start | bytes 24580
  69.1 32.5 %collective-permute-start.3 = (bf16[256,512]{1,0:T(8,128)(2,1)S(1)}, bf16[256,512]{1,0:T(8,128)(2,1)S(1)}, u32[]{:S(2)}, u32[]{:S(2)}) collective-permute-start(bf16[256,512]{1,0:T(8,128)(2,1)S(1)} %get-tuple-element.37), channel_id=1, source_target_pairs={{0,1},{1,2},{2,3},{3,0},{4,5},{5,6},{6,7},{7,4},{8,9},{9,10},{10,1... | collective-permute-start | bytes 786440 | tf_op jit(solution)/shard_map/ppermute | solution.py:693
  70.9 30.7 %collective-permute-start.4 = (bf16[256,512]{1,0:T(8,128)(2,1)S(1)}, bf16[256,512]{1,0:T(8,128)(2,1)S(1)}, u32[]{:S(2)}, u32[]{:S(2)}) collective-permute-start(bf16[256,512]{1,0:T(8,128)(2,1)S(1)} %get-tuple-element.38), channel_id=1, source_target_pairs={{0,2},{1,3},{2,0},{3,1},{4,6},{5,7},{6,4},{7,5},{8,10},{9,11},{10,... | collective-permute-start | bytes 786440 | tf_op jit(solution)/shard_map/ppermute | solution.py:693
  74.2 27.4 %collective-permute-start.5 = (bf16[256,512]{1,0:T(8,128)(2,1)S(1)}, bf16[256,512]{1,0:T(8,128)(2,1)S(1)}, u32[]{:S(2)}, u32[]{:S(2)}) collective-permute-start(bf16[256,512]{1,0:T(8,128)(2,1)S(1)} %get-tuple-element.39), channel_id=1, source_target_pairs={{0,3},{1,0},{2,1},{3,2},{4,7},{5,4},{6,5},{7,6},{8,11},{9,8},{10,9... | collective-permute-start | bytes 786440 | tf_op jit(solution)/shard_map/ppermute | solution.py:693
  90.6 16.1 %all-to-all-start.3 = ((f32[128,1,128]{2,1,0:T(1,128)}), f32[128,1,128]{2,1,0:T(1,128)S(1)}, u32[]{:S(2)}, u32[]{:S(2)}) async-start(f32[128,1,128]{2,1,0:T(1,128)} %head_kernel.1), calls=%async_computation.3 | async-start | bytes 131072 | tf_op jit(solution)/shard_map/all_to_all | solution.py:676
